TPU v7x, 512 devices: a whole 4x4x16 slice. The times are simulated.
512 devices in a mesh: row: 16 (over x, y), col: 32 (over z, core).
Axes of the slice: x: 4, y: 4, z: 16, core: 2. Of those that a mesh axis runs over, the one named last changes fastest.
Arguments:
- diag_block: float32 [512, 512], P('row', 'col'), as said below
- panel: float32 [14336, 512], P(('row', 'col')), may hold values from -0.625 to 0.625
- trailing: float32 [14336, 14336], P('row', 'col'), may hold values from -6 to 6
- truth_panel: float32 [5120, 512], P('row', 'col'), may hold values from -0.625 to 0.625
- truth_rest: float32 [5120, 14336], P('row', 'col'), may hold values from -6 to 6
Outputs:
- factor: float32 [14336, 512], P(('row', 'col'))
- updated: float32 [14336, 14336], P('row', 'col')
- solved: float32 [5120, 512], P('row', 'col')
- truth_updated: float32 [5120, 14336], P('row', 'col')
Inputs may be any that keep to these rules, and one draw needn't show every extreme that they name: diag_block is symmetric positive definite.
All inputs are finite; a program needn't handle non-finite values.
Results may differ from a plain program's by a relative error of at most 0.00014.
Values sent between devices are 32-bit elements; how exact they have to be, the bound alone decides.
No kernel may reach another device: no remote copies, remote signals or barrier semaphores. Data moves between devices by JAX's collectives and lax.ppermute only.
A program may use at most 64 MiB of HBM per device.

v0:
```python
import jax
import jax.numpy as jnp
from jax import lax
from jax.sharding import PartitionSpec as P

precise = lax.Precision.HIGHEST


def right_solve(lower_factor, right_side):
    return jax.scipy.linalg.solve_triangular(lower_factor, right_side.T, lower=True).T


def outer_rows(left_rows, dealt_rows):
    return lax.dot_general(left_rows, dealt_rows, (((1,), (1,)), ((), ())), precision=precise)


def per_device(diag_block, panel, trailing, truth_panel, truth_rest):
    stacked = lax.all_gather(diag_block, "row", axis=0, tiled=True)
    whole_block = lax.all_gather(stacked, "col", axis=1, tiled=True)
    lower_factor = jnp.linalg.cholesky(whole_block)
    factor = right_solve(lower_factor, panel)
    dealt_rows = lax.all_gather(factor, "row", axis=0, tiled=True)
    updated = trailing - outer_rows(lax.all_gather(factor, "col", axis=0, tiled=True), dealt_rows)
    full_rows = lax.all_gather(truth_panel, "col", axis=1, tiled=True)
    solved_all = right_solve(lower_factor, full_rows)
    columns = truth_panel.shape[1]
    solved = lax.dynamic_slice_in_dim(solved_all, lax.axis_index("col") * columns, columns, 1)
    truth_updated = truth_rest - outer_rows(solved_all, dealt_rows)
    return (factor, updated, solved, truth_updated)


def solution(mesh):
    in_specs = (
        P("row", "col"),
        P(("row", "col"), None),
        P("row", "col"),
        P("row", "col"),
        P("row", "col"),
    )
    out_specs = (P(("row", "col"), None), P("row", "col"), P("row", "col"), P("row", "col"))
    return jax.shard_map(
        per_device, mesh=mesh, in_specs=in_specs, out_specs=out_specs, check_vma=False
    )
```

profile of v0, /device:TPU:1, one launch (start us, length us, event | category | flops | bytes accessed | tf_op | source)
XLA Modules:
  0.0 336.7 jit_solution(1454853672951744983)
XLA Ops:
  7.2 19.6 %all-gather = f32[16,32,16]{1,2,0:T(8,128)S(1)} all-gather(f32[1,32,16]{1,2,0:T(8,128)} %bitcast.79), channel_id=1, replica_groups=mesh['row'=16,'col'=32] {'row'}, dimensions={0}, use_global_device_ids=true | all-gather | bytes 34816 | tf_op jit(solution)/shard_map/all_gather | solution.py:18
  27.7 78.7 %all-gather.6.cloned.1.call-done = f32[512,512]{0,1:T(8,128)} async-done(((f32[512,16]{0,1:T(8,128)}), f32[512,512]{0,1:T(8,128)}) %all-gather.6.cloned.1.call-update) | async-done | bytes 1048592 | tf_op jit(solution)/shard_map/all_gather | solution.py:19
  106.4 1.6 copy.20
  108.3 11.7 %cholesky.104 = f32[128,128]{1,0:T(8,128)S(1)} custom-call(f32[128,128]{1,0:T(8,128)S(1)} %cholesky.266), custom_call_target="Cholesky" | custom-call | tf_op jit(solution)/shard_map/jit(cholesky)/cholesky | solution.py:20
  120.1 9.8 %custom-call.34 = f32[1,128,128]{1,2,0:T(8,128)S(1)} custom-call(f32[1,128,128]{2,1,0:T(8,128)S(1)} %get-tuple-element.49), custom_call_target="InvertDiagBlocksLowerTriangular" | custom-call | tf_op jit(solution)/shard_map/jit(cholesky)/cholesky | solution.py:20
  130.7 11.7 %cholesky.217 = f32[128,128]{1,0:T(8,128)S(1)} custom-call(f32[128,128]{1,0:T(8,128)S(1)} %cholesky.270), custom_call_target="Cholesky" | custom-call | tf_op jit(solution)/shard_map/jit(cholesky)/cholesky | solution.py:20
  142.4 18.5 %custom-call.35 = f32[1,128,128]{1,2,0:T(8,128)S(1)} custom-call(f32[1,128,128]{2,1,0:T(8,128)S(1)} %get-tuple-element.46), custom_call_target="InvertDiagBlocksLowerTriangular" | custom-call | tf_op jit(solution)/shard_map/jit(cholesky)/cholesky | solution.py:20
  161.6 11.7 %cholesky.238 = f32[128,128]{1,0:T(8,128)S(1)} custom-call(f32[128,128]{1,0:T(8,128)S(1)} %cholesky.275), custom_call_target="Cholesky" | custom-call | tf_op jit(solution)/shard_map/jit(cholesky)/cholesky | solution.py:20
  174.0 9.8 %custom-call.36 = f32[1,128,128]{1,2,0:T(8,128)S(1)} custom-call(f32[1,128,128]{2,1,0:T(8,128)S(1)} %get-tuple-element.43), custom_call_target="InvertDiagBlocksLowerTriangular" | custom-call | tf_op jit(solution)/shard_map/jit(cholesky)/cholesky | solution.py:20
  184.4 11.7 %cholesky.255 = f32[128,128]{1,0:T(8,128)S(1)} custom-call(f32[128,128]{1,0:T(8,128)S(1)} %convolution_subtract_fusion.7), custom_call_target="Cholesky" | custom-call | tf_op jit(solution)/shard_map/jit(cholesky)/cholesky | solution.py:20
  200.3 10.5 %while.1 = (s32[]{:T(128)}, f32[512,512]{1,0:T(8,128)S(1)}, s32[4,2]{0,1:T(2,128)S(1)}, f32[4,128,128]{2,1,0:T(8,128)}, s32[]{:T(128)}) while((s32[]{:T(128)}, f32[512,512]{1,0:T(8,128)S(1)}, s32[4,2]{0,1:T(2,128)S(1)}, f32[4,128,128]{2,1,0:T(8,128)}, s32[]{:T(128)}) %tuple.36), condition=%wide.while_cond, body=%wide.while_body.sunk | while | flops 2 | bytes 132705 | solution.py:10
  200.9 2.0 bitcast_dynamic-update-slice_fusion.2
  203.6 2.0 bitcast_dynamic-update-slice_fusion.2
  206.2 2.0 bitcast_dynamic-update-slice_fusion.2
  208.8 2.0 bitcast_dynamic-update-slice_fusion.2
  210.8 40.1 %custom-call.37 = f32[4,128,128]{1,2,0:T(8,128)S(1)} custom-call(f32[4,128,128]{2,1,0:T(8,128)} %get-tuple-element.11), custom_call_target="InvertDiagBlocksLowerTriangular" | custom-call | tf_op jit(solution)/shard_map/jit(_solve_triangular)/triangular_solve | solution.py:10
  253.2 31.7 %all_gather.19 = f32[320,512]{0,1:T(8,128)S(1)} all-gather(f32[320,16]{0,1:T(8,128)S(1)} %copy-done.3), channel_id=1, replica_groups=mesh['row'=16,'col'=32] {'col'}, dimensions={1}, use_global_device_ids=true | all-gather | bytes 675840 | tf_op jit(solution)/shard_map/all_gather | solution.py:24
  285.9 21.7 %all-gather.2 = f32[16,28,512]{2,1,0:T(8,128)S(1)} all-gather(f32[1,28,512]{2,1,0:T(8,128)S(1)} %copy-done.1), channel_id=1, replica_groups=mesh['row'=16,'col'=32] {'row'}, dimensions={0}, use_global_device_ids=true | all-gather | bytes 974848 | tf_op jit(solution)/shard_map/all_gather | solution.py:22
  310.4 1.4 convolution_subtract_fusion.4
  312.1 1.5 convolution_subtract_fusion.3
  314.8 3.2 convolution_subtract_fusion.1
  317.9 4.3 %all-gather.8.cloned.1.call-done = f32[32,28,512]{2,1,0:T(8,128)} async-done(((f32[1,28,512]{2,1,0:T(8,128)}), f32[32,28,512]{2,1,0:T(8,128)}) %all-gather.8.cloned.1.call-update) | async-done | bytes 1835024 | tf_op jit(solution)/shard_map/all_gather | solution.py:23
  322.2 1.6 reshape.81
  323.9 5.7 %convolution_subtract_fusion = f32[896,448]{0,1:T(8,128)} fusion(f32[896,448]{0,1:T(8,128)} %param.7, f32[896,512]{1,0:T(8,128)S(1)} %reshape.81, f32[448,512]{1,0:T(8,128)S(1)} %reshape.83), kind=kOutput, calls=%fused_computation.2 | convolution fusion | flops 2466652160 | bytes 5963776 | tf_op jit(solution)/shard_map/dot_general | solution.py:14
  (62 shorter events, 15.4 us)
Async XLA Ops:
  7.2 99.2 %all-gather.6.cloned.1.call-start = ((), (), s32[]{:S(2)}) async-start(), calls=%async_computation | async-start | bytes 1081344 | tf_op jit(solution)/shard_map/all_gather | solution.py:19
  27.6 294.6 %all-gather.8.cloned.1.call-start = ((), (), s32[]{:S(2)}) async-start(), calls=%async_computation.1 | async-start | bytes 2162688 | tf_op jit(solution)/shard_map/all_gather | solution.py:23
  106.4 1.7 copy-start
  173.3 77.6 %copy-start.2 = (f32[28,512]{1,0:T(8,128)S(1)}, f32[28,512]{1,0:T(8,128)}, u32[]{:S(2)}) copy-start(f32[28,512]{1,0:T(8,128)} %param.6) | copy-start | bytes 172036
  200.0 53.1 %copy-start.3 = (f32[320,16]{0,1:T(8,128)S(1)}, f32[320,16]{0,1:T(8,128)}, u32[]{:S(2)}) copy-start(f32[320,16]{0,1:T(8,128)} %param.8) | copy-start | bytes 61444
  253.1 32.8 %copy-start.1 = (f32[1,28,512]{2,1,0:T(8,128)S(1)}, f32[1,28,512]{2,1,0:T(8,128)}, u32[]{:S(2)}) copy-start(f32[1,28,512]{2,1,0:T(8,128)} %get-tuple-element.38) | copy-start | bytes 172036
Sparse Core Ops, SparseCore 0:
  27.8 78.5 all-gather.5
  253.3 68.9 all-gather.7
where the time goes:
time: 342 us; the launch traced here: 337 us
  other arithmetic  128 us (37%)
  waiting for transfers between devices  83 us (24%)
  blocking collectives  73 us (21%)
  matrix products  18.3 us (5%)
  between operations  17.3 us (5%)
  local copies, waits for them, and re-layouts  16.6 us (5%)
    another operation x14, other arithmetic, per_device(): lower_factor = jnp.linalg.cholesky(whole_block)  87.1 us
    all_gather x1, waiting for transfers between devices, per_device(): whole_block = lax.all_gather(stacked, 'col', axis=1, tiled=True)  78.7 us
    another operation x4, other arithmetic, right_solve(): jax.scipy.linalg.solve_triangular(lower_factor, right_side.T, lower=True)  40.5 us
    all_gather x1, blocking collectives, per_device(): full_rows = lax.all_gather(truth_panel, 'col', axis=1, tiled=True)  31.7 us
    all_gather x1, blocking collectives, per_device(): dealt_rows = lax.all_gather(factor, 'row', axis=0, tiled=True)  21.7 us
    all_gather x1, blocking collectives, per_device(): stacked = lax.all_gather(diag_block, 'row', axis=0, tiled=True)  19.6 us
    another operation x12, local copies, waits for them, and re-layouts  10.4 us
    dot_general x2, matrix products, outer_rows(): lax.dot_general(left_rows, dealt_rows, (((1,), (1,)), ((), ())), precisio...  8.82 us
  transfers between devices with their start and end apart: 2, of which 2 were waited for; matrix products, arithmetic and copies ran while one was open for 3% of the time, Pallas kernels for 0%

commit v1 on v0

v1 whole, which is shorter than its diff:
```python
import jax
import jax.numpy as jnp
from jax import lax
from jax.experimental import pallas as pl
from jax.experimental.pallas import tpu as pltpu
from jax.sharding import PartitionSpec as P
HI = lax.Precision.HIGHEST
NT = (((1,), (1,)), ((), ()))
NN = (((1,), (0,)), ((), ()))

def factor_tile(d_ref, o_ref):
    n = 16
    lane = lax.broadcasted_iota(jnp.int32, (8, 128), 1)
    sub = lax.broadcasted_iota(jnp.int32, (8, 128), 0)
    full = lambda v: jnp.broadcast_to(v, (8, 128))
    m = [d_ref[8 * i:8 * i + 8, :] for i in range(n)]
    for j in range(n):
        lo = 8 * j
        here = (lane >= lo) & (lane < lo + 8)
        own = m[j]
        cols = [full(own[:, lo + c:lo + c + 1]) for c in range(8)]
        s = {(a, c): full(cols[c][a:a + 1, :]) for c in range(8) for a in range(c, 8)}
        rows = jnp.where(here, jnp.where(lane - lo == sub, 1.0, 0.0), own)
        r = [full(rows[a:a + 1, :]) for a in range(8)]
        l, inv, u = {}, [], []
        for c in range(8):
            q = lax.rsqrt(s[c, c])
            inv.append(q)
            for a in range(c + 1, 8):
                l[a, c] = s[a, c] * q
            for a in range(c + 1, 8):
                for b in range(c + 1, a + 1):
                    s[a, b] = s[a, b] - l[a, c] * l[b, c]
            u.append(r[c] * q)
            for a in range(c + 1, 8):
                r[a] = r[a] - l[a, c] * u[c]
        done = u[0]
        for a in range(1, 8):
            done = jnp.where(sub == a, u[a], done)
        o_ref[lo:lo + 8, :] = jnp.where(lane < lo + 8, done, 0.0)
        for i in range(j + 1, n):
            b = [full(m[i][:, lo + c:lo + c + 1]) for c in range(8)]
            acc = jnp.where(here, 0.0, m[i])
            for c in range(8):
                t = b[c] * inv[c]
                for e in range(c + 1, 8):
                    b[e] = b[e] - t * l[e, c]
                acc = acc - t * u[c]
            m[i] = acc

def chol_kernel(a_ref, o_ref, m_ref, d_ref, t_ref, u_ref):
    nb = 128
    n = a_ref.shape[0]
    m_ref[...] = a_ref[...]
    col = lax.broadcasted_iota(jnp.int32, (nb, n), 1)
    row = lax.broadcasted_iota(jnp.int32, (n, nb), 0)

    def step(k, _):
        at = pl.ds(pl.multiple_of(k * nb, nb), nb)
        d_ref[...] = m_ref[at, at]
        factor_tile(d_ref, t_ref)
        t = t_ref[...]
        left = lax.dot_general(m_ref[:, at], t, NT, precision=HI, preferred_element_type=jnp.float32)
        left = jnp.where(row >= (k + 1) * nb, left, 0.0)
        u_ref[...] = lax.dot_general(t, m_ref[at, :], NN, precision=HI, preferred_element_type=jnp.float32)
        u_ref[:, at] = t
        m_ref[:, at] = jnp.where(row >= (k + 1) * nb, 0.0, m_ref[:, at])
        m_ref[...] = m_ref[...] - lax.dot_general(left, u_ref[...], NN, precision=HI, preferred_element_type=jnp.float32)
        m_ref[at, :] = jnp.where(col < (k + 1) * nb, u_ref[...], 0.0)
        return 0
    lax.fori_loop(0, n // nb, step, 0)
    o_ref[...] = m_ref[...]


def invert_factor(block):
    n = block.shape[0]
    return pl.pallas_call(
        chol_kernel,
        out_shape=jax.ShapeDtypeStruct((n, n), jnp.float32),
        in_specs=[pl.BlockSpec(memory_space=pltpu.VMEM)],
        out_specs=pl.BlockSpec(memory_space=pltpu.VMEM),
        scratch_shapes=[
            pltpu.VMEM((n, n), jnp.float32),
            pltpu.VMEM((128, 128), jnp.float32),
            pltpu.VMEM((128, 128), jnp.float32),
            pltpu.VMEM((128, n), jnp.float32),
        ],
        cost_estimate=pl.CostEstimate(flops=10**10, bytes_accessed=2 * 10**6, transcendentals=0),
        name="invert_factor",
    )(block)


def spread(value, axes, count):
    copies = jnp.broadcast_to(value[None], (count,) + value.shape)
    return lax.all_to_all(copies, axes, 0, 0)


HIGH = lax.Precision.HIGH


def per_device(diag_block, panel, trailing, truth_panel, truth_rest):
    rows, columns = ("x", "y"), ("z", "k")
    packed = jnp.concatenate(
        [
            jnp.pad(panel, ((0, 4), (0, 0))),
            jnp.pad(truth_panel.T, ((0, 0), (0, 192))),
        ],
        0,
    )
    gathered = lax.all_gather(packed, columns, axis=0, tiled=False)
    pieces = spread(diag_block.reshape(4, 128), columns, 32)
    strip = pieces.reshape(32, 4, 8, 16).transpose(1, 2, 0, 3).reshape(32, 512)
    whole = spread(strip, rows, 16).reshape(512, 512)
    dealt = spread(panel, rows, 16).reshape(448, 512)
    inverse = invert_factor(whole)
    factor = lax.dot_general(panel, inverse, NT, precision=HI)
    dealt_rows = lax.dot_general(dealt, inverse, NT, precision=HIGH)
    own_rows = gathered[:, :28, :].reshape(896, 512)
    factor_rows = lax.dot_general(own_rows, inverse, NT, precision=HIGH)
    updated = trailing - lax.dot_general(factor_rows, dealt_rows, NT, precision=HIGH)
    truth_rows = gathered[:, 32:, :320].reshape(512, 320)
    solved_all = lax.dot_general(truth_rows, inverse, (((0,), (1,)), ((), ())), precision=HIGH)
    at = (lax.axis_index("z") * 2 + lax.axis_index("k")) * 16
    solved = lax.dynamic_slice_in_dim(solved_all, at, 16, 1)
    truth_updated = truth_rest - lax.dot_general(solved_all, dealt_rows, NT, precision=HIGH)
    return factor, updated, solved, truth_updated


def solution(mesh):
    fine = jax.sharding.Mesh(mesh.devices.reshape(4, 4, 16, 2), ("x", "y", "z", "k"))
    rows, columns = ("x", "y"), ("z", "k")
    tiled, whole = P(rows, columns), P(rows + columns, None)
    return jax.shard_map(
        per_device,
        mesh=fine,
        in_specs=(tiled, whole, tiled, tiled, tiled),
        out_specs=(whole, tiled, tiled, tiled),
        check_vma=False,
    )
```

time: 342 us -> 142 us (0.42); the launches traced: 337 us -> 141 us
  other arithmetic: 128 us -> 1.51 us
  waiting for transfers between devices: 83 us -> 28.9 us
  blocking collectives: 73 us -> 29.6 us
  Pallas kernels: 0 us -> 27.4 us
  starting transfers between devices: 0.08 us -> 11.1 us
  local copies, waits for them, and re-layouts: 16.6 us -> 11.8 us
    another operation x18 -> x0, other arithmetic: 128 us -> none  [the longest x14 87.1 us: per_device(): lower_factor = jnp.linalg.cholesky(whole_block)]
    all_gather x2 -> x1, waiting for transfers between devices: 83 us -> 0.01 us  [per_device(): gathered = lax.all_gather(packed, columns, axis=0, tiled=False)]
    all_gather x3 -> x0, blocking collectives: 73 us -> none  [the longest x1 31.7 us: per_device(): full_rows = lax.all_gather(truth_panel, 'col', axis=1, tiled=True)]
    all_to_all x0 -> x1, blocking collectives: none -> 29.6 us  [spread(): return lax.all_to_all(copies, axes, 0, 0)]
    all_to_all x0 -> x2, waiting for transfers between devices: none -> 28.9 us  [spread(): return lax.all_to_all(copies, axes, 0, 0)]
    pallas_call x0 -> x1, Pallas kernels: none -> 27.4 us  [invert_factor(): pl.pallas_call(chol_kernel, out_shape=jax.ShapeDtypeStruct((n, n), jnp.fl...]
    all_to_all x0 -> x2, starting transfers between devices: none -> 11.1 us  [spread(): return lax.all_to_all(copies, axes, 0, 0)]
    another operation x17 -> x0, local copies, waits for them, and re-layouts: 10.6 us -> none
  transfers between devices with their start and end apart: 2 -> 3, of which waited for: 2 -> 2; matrix products, arithmetic and copies ran while one was open for 3% -> 7% of each run, Pallas kernels for 0% -> 19%
where the time goes in v1:
time: 142 us; the launch traced here: 141 us
  blocking collectives  29.6 us (21%)
  waiting for transfers between devices  28.9 us (20%)
  Pallas kernels  27.4 us (19%)
  matrix products  16.2 us (11%)
  between operations  14.1 us (10%)
  local copies, waits for them, and re-layouts  11.8 us (8%)
  starting transfers between devices  11.1 us (8%)
  other arithmetic  1.51 us (1%)
    all_to_all x1, blocking collectives, spread(): return lax.all_to_all(copies, axes, 0, 0)  29.6 us
    all_to_all x2, waiting for transfers between devices, spread(): return lax.all_to_all(copies, axes, 0, 0)  28.9 us
    pallas_call x1, Pallas kernels, invert_factor(): pl.pallas_call(chol_kernel, out_shape=jax.ShapeDtypeStruct((n, n), jnp.fl...  27.4 us
    all_to_all x2, starting transfers between devices, spread(): return lax.all_to_all(copies, axes, 0, 0)  11.1 us
    dot_general x1, matrix products, per_device(): lax.dot_general(factor_rows, dealt_rows, NT, precision=HIGH)  4.21 us
    broadcast_in_dim x5, local copies, waits for them, and re-layouts, spread(): copies = jnp.broadcast_to(value[None], (count,) + value.shape)  3.4 us
    dot_general x1, matrix products, per_device(): factor = lax.dot_general(panel, inverse, NT, precision=HI)  2.98 us
    dot_general x1, matrix products, per_device(): factor_rows = lax.dot_general(own_rows, inverse, NT, precision=HIGH)  2.91 us
  transfers between devices with their start and end apart: 3, of which 2 were waited for; matrix products, arithmetic and copies ran while one was open for 7% of the time, Pallas kernels for 19%

profile of v1, /device:TPU:1, one launch (start us, length us, event | category | flops | bytes accessed | tf_op | source)
XLA Modules:
  0.0 140.5 jit_solution(366865592118667802)
XLA Ops:
  7.2 1.5 %select_maximum_fusion = f32[48,512]{1,0:T(8,128)} fusion(f32[16,320]{1,0:T(8,128)} %bitcast.26, f32[28,512]{1,0:T(8,128)} %param.6), kind=kLoop, calls=%fused_computation.2 | loop fusion | flops 122880 | bytes 176128 | tf_op jit(solution)/shard_map/concatenate | solution.py:103
  8.7 0.8 copy.13
  9.6 29.6 %all_to_all.15 = f32[32,4,128]{2,1,0:T(4,128)S(1)} all-to-all(f32[32,4,128]{2,1,0:T(4,128)S(1)} %broadcast_in_dim.21), channel_id=1, replica_groups=mesh['x'=4,'y'=4,'z'=16,'k'=2] {'z','k'}, dimensions={0} | all-to-all | bytes 131072 | tf_op jit(solution)/shard_map/all_to_all | solution.py:95
  39.2 1.9 %broadcast_in_dim.24 = f32[16,28,512]{2,1,0:T(8,128)} broadcast(f32[28,512]{1,0:T(8,128)} %param.6), dimensions={1,2} | broadcast | bytes 974848 | tf_op jit(solution)/shard_map/broadcast_in_dim | solution.py:94
  41.1 6.8 %all-to-all-start.2 = ((f32[16,28,512]{2,1,0:T(8,128)}), f32[16,28,512]{2,1,0:T(8,128)S(1)}, u32[]{:S(2)}, u32[]{:S(2)}) async-start(f32[16,28,512]{2,1,0:T(8,128)} %broadcast_in_dim.24), calls=%async_computation.2 | async-start | bytes 2097152 | tf_op jit(solution)/shard_map/all_to_all | solution.py:95
  47.9 0.1 copy.14
  48.0 0.2 copy.15
  48.2 0.3 broadcast_in_dim.22
  48.5 14.4 %all-to-all-done.2 = f32[16,28,512]{2,1,0:T(8,128)S(1)} async-done(((f32[16,28,512]{2,1,0:T(8,128)}), f32[16,28,512]{2,1,0:T(8,128)S(1)}, u32[]{:S(2)}, u32[]{:S(2)}) %all-to-all-start.2) | async-done | bytes 917536 | tf_op jit(solution)/shard_map/all_to_all | solution.py:95
  62.9 1.1 broadcast_in_dim.23
  64.0 4.3 %all-to-all-start.1 = ((f32[16,32,512]{2,1,0:T(8,128)}), f32[16,32,512]{2,1,0:T(8,128)S(1)}, u32[]{:S(2)}, u32[]{:S(2)}) async-start(f32[16,32,512]{2,1,0:T(8,128)} %broadcast_in_dim.23), calls=%async_computation.1 | async-start | bytes 2097152 | tf_op jit(solution)/shard_map/all_to_all | solution.py:95
  68.4 14.5 %all-to-all-done.1 = f32[16,32,512]{2,1,0:T(8,128)S(1)} async-done(((f32[16,32,512]{2,1,0:T(8,128)}), f32[16,32,512]{2,1,0:T(8,128)S(1)}, u32[]{:S(2)}, u32[]{:S(2)}) %all-to-all-start.1) | async-done | bytes 1048608 | tf_op jit(solution)/shard_map/all_to_all | solution.py:95
  82.9 1.0 copy-done.4
  83.9 27.4 %invert_factor.1 = f32[512,512]{1,0:T(8,128)} custom-call(f32[512,512]{1,0:T(8,128)} %bitcast.25), custom_call_target="tpu_custom_call" | custom-call | flops 10000000000 | bytes 2000000 | tf_op jit(solution)/shard_map/invert_factor/pallas_call | solution.py:77
  111.3 3.0 %fusion = f32[28,512]{1,0:T(8,128)} fusion(f32[28,512]{1,0:T(8,128)S(1)} %copy-done.6, f32[512,512]{1,0:T(8,128)} %invert_factor.1), kind=kOutput, calls=%fused_computation.6 | convolution fusion | flops 88080384 | bytes 1163264 | tf_op jit(solution)/shard_map/dot_general | solution.py:116
  114.2 1.9 %fusion.2 = f32[448,512]{1,0:T(8,128)} fusion(f32[448,512]{1,0:T(8,128)S(1)} %reshape.29, f32[512,512]{1,0:T(8,128)S(1)} %copy-done), kind=kOutput, calls=%fused_computation.8 | convolution fusion | flops 704643072 | bytes 2883584 | tf_op jit(solution)/shard_map/dot_general | solution.py:117
  116.1 2.1 %slice.9 = f32[32,16,320]{2,1,0:T(8,128)} slice(f32[32,48,512]{2,1,0:T(8,128)} %bitcast.22), slice={[0:32], [32:48], [0:320]} | slice | bytes 1310720 | tf_op jit(solution)/shard_map/slice | solution.py:121
  118.2 1.8 %slice.8 = f32[32,28,512]{2,1,0:T(8,128)S(1)} slice(f32[32,48,512]{2,1,0:T(8,128)} %bitcast.23), slice={[0:32], [0:28], [0:512]} | slice | bytes 3670016 | tf_op jit(solution)/shard_map/slice | solution.py:118
  120.0 1.5 %reshape.28 = f32[896,512]{1,0:T(8,128)} reshape(f32[32,28,512]{2,1,0:T(8,128)S(1)} %slice.8) | data formatting | bytes 3670016 | tf_op jit(solution)/shard_map/reshape | solution.py:118
  121.5 2.7 %fusion.3 = f32[320,512]{1,0:T(8,128)S(1)} fusion(f32[512,320]{1,0:T(8,128)} %bitcast.21, f32[512,512]{1,0:T(8,128)S(1)} %copy-done), kind=kOutput, calls=%fused_computation.9 | convolution fusion | flops 503316480 | bytes 2359296 | tf_op jit(solution)/shard_map/dot_general | solution.py:122
  124.2 2.9 %fusion.1 = f32[896,512]{1,0:T(8,128)} fusion(f32[896,512]{1,0:T(8,128)S(1)} %copy-done.3, f32[512,512]{1,0:T(8,128)S(1)} %copy-done), kind=kOutput, calls=%fused_computation.7 | convolution fusion | flops 1409286144 | bytes 4718592 | tf_op jit(solution)/shard_map/dot_general | solution.py:119
  127.2 0.7 copy.16
  127.9 1.5 %convolution_subtract_fusion.1 = f32[320,448]{1,0:T(8,128)} fusion(f32[320,448]{1,0:T(8,128)S(1)} %copy-done.5, f32[320,512]{1,0:T(8,128)S(1)} %fusion.3, f32[448,512]{1,0:T(8,128)S(1)} %copy-done.1), kind=kOutput, calls=%fused_computation.1 | convolution fusion | flops 440545280 | bytes 2719744 | tf_op jit(solution)/shard_map/dot_general | solution.py:125
  129.5 4.2 %convolution_subtract_fusion = f32[896,448]{0,1:T(8,128)} fusion(f32[896,448]{0,1:T(8,128)} %param.7, f32[896,512]{1,0:T(8,128)S(1)} %copy-done.2, f32[448,512]{1,0:T(8,128)S(1)} %copy-done.1), kind=kOutput, calls=%fused_computation | convolution fusion | flops 1233526784 | bytes 5963776 | tf_op jit(solution)/shard_map/dot_general | solution.py:120
  (20 shorter events, 0.4 us)
Async XLA Ops:
  7.2 108.9 %all-gather.3.cloned.1.call-start = ((), (), s32[]{:S(2)}) async-start(), calls=%async_computation.3 | async-start | bytes 3244032 | tf_op jit(solution)/shard_map/all_gather | solution.py:110
  41.1 21.8 %all-to-all-start.2 = ((f32[16,28,512]{2,1,0:T(8,128)}), f32[16,28,512]{2,1,0:T(8,128)S(1)}, u32[]{:S(2)}, u32[]{:S(2)}) async-start(f32[16,28,512]{2,1,0:T(8,128)} %broadcast_in_dim.24), calls=%async_computation.2 | async-start | bytes 2097152 | tf_op jit(solution)/shard_map/all_to_all | solution.py:95
  64.0 18.9 %all-to-all-start.1 = ((f32[16,32,512]{2,1,0:T(8,128)}), f32[16,32,512]{2,1,0:T(8,128)S(1)}, u32[]{:S(2)}, u32[]{:S(2)}) async-start(f32[16,32,512]{2,1,0:T(8,128)} %broadcast_in_dim.23), calls=%async_computation.1 | async-start | bytes 2097152 | tf_op jit(solution)/shard_map/all_to_all | solution.py:95
  82.9 1.0 copy-start.4
  83.9 27.4 %copy-start.6 = (f32[28,512]{1,0:T(8,128)S(1)}, f32[28,512]{1,0:T(8,128)}, u32[]{:S(2)}) copy-start(f32[28,512]{1,0:T(8,128)} %param.6) | copy-start | bytes 172036
  111.2 3.0 %copy-start = (f32[512,512]{1,0:T(8,128)S(1)}, f32[512,512]{1,0:T(8,128)}, u32[]{:S(2)}) copy-start(f32[512,512]{1,0:T(8,128)} %invert_factor.1) | copy-start | bytes 3145732
  121.5 2.7 %copy-start.3 = (f32[896,512]{1,0:T(8,128)S(1)}, f32[896,512]{1,0:T(8,128)}, u32[]{:S(2)}) copy-start(f32[896,512]{1,0:T(8,128)} %reshape.28) | copy-start | bytes 5505028
  124.1 3.8 %copy-start.1 = (f32[448,512]{1,0:T(8,128)S(1)}, f32[448,512]{1,0:T(8,128)}, u32[]{:S(2)}) copy-start(f32[448,512]{1,0:T(8,128)} %fusion.2) | copy-start | bytes 2752516
  124.2 3.8 %copy-start.5 = (f32[320,448]{1,0:T(8,128)S(1)}, f32[320,448]{1,0:T(8,128)}, u32[]{:S(2)}) copy-start(f32[320,448]{1,0:T(8,128)} %param.9) | copy-start | bytes 1720324
  127.9 1.5 %copy-start.2 = (f32[896,512]{1,0:T(8,128)S(1)}, f32[896,512]{1,0:T(8,128)}, u32[]{:S(2)}) copy-start(f32[896,512]{1,0:T(8,128)} %fusion.1) | copy-start | bytes 5505028
Sparse Core Ops, SparseCore 0:
  10.7 78.2 all-gather.2

commit v2 on v1

--- a/solution.py
+++ b/solution.py
@@ -95,7 +95,123 @@
     return lax.all_to_all(copies, axes, 0, 0)
 
 
-HIGH = lax.Precision.HIGH
+def halves(value):
+    high = value.astype(jnp.bfloat16)
+    return high, (value - high.astype(jnp.float32)).astype(jnp.bfloat16)
+
+
+def thrice(a_high, a_low, b_high, b_low, dims):
+    dot = lambda p, q: lax.dot_general(p, q, dims, preferred_element_type=jnp.float32)
+    return dot(a_high, b_high) + dot(a_high, b_low) + dot(a_low, b_high)
+
+
+def apply_kernel(
+    col_ref, inv_hbm, dealt_hbm, gathered_hbm, panel_hbm, trailing_hbm, rest_hbm,
+    factor_hbm, updated_hbm, solved_hbm, truth_hbm,
+    inv, dealt, gathered, panel, trailing, rest,
+    inv_high, inv_low, row_high, row_low, x_high, x_low, factor, solved, sem, out_sem,
+):
+    loads = [
+        pltpu.make_async_copy(src, dst, sem.at[i])
+        for i, (src, dst) in enumerate(
+            [
+                (inv_hbm, inv), (dealt_hbm, dealt), (gathered_hbm, gathered),
+                (panel_hbm, panel), (trailing_hbm, trailing), (rest_hbm, rest),
+            ]
+        )
+    ]
+    for load in loads:
+        load.start()
+    loads[0].wait()
+    inv_high[...], inv_low[...] = halves(inv[...])
+
+    def solve(high, low):
+        a = thrice(high[:, :256], low[:, :256], inv_high[:256, :256], inv_low[:256, :256], NT)
+        b = thrice(high, low, inv_high[256:, :], inv_low[256:, :], NT)
+        return jnp.concatenate([a, b], 1)
+
+    loads[1].wait()
+    for r in range(16):
+        row_high[28 * r:28 * r + 28, :] = dealt[r]
+    high, low = halves(row_high[...])
+    done = solve(high, low)
+    d_high, d_low = halves(done)
+    loads[2].wait()
+    loads[3].wait()
+    stack = row_low
+    for c in range(32):
+        stack[28 * c:28 * c + 28, :] = gathered[c, 0:28, :]
+    truth = gathered[:, 32:48, 0:384].reshape(512, 384)
+    stack[896:1216, :] = truth.T[0:320, :]
+    stack[1216:1244, :] = panel[...]
+    stack[1244:1248, :] = jnp.zeros((4, 512), jnp.float32)
+    at = pl.ds(pl.multiple_of(col_ref[0] * 16, 16), 16)
+    i_high, i_low = halves(inv[at, :])
+    t_high, t_low = halves(stack[896:1216, :])
+    solved[...] = thrice(i_high, i_low, t_high, t_low, NT)
+    for lo, hi in ((0, 416), (416, 832), (832, 1248)):
+        high, low = halves(stack[lo:hi, :])
+        part = solve(high, low)
+        if hi == 1248:
+            factor[...] = part[1216 - lo:1244 - lo, :]
+        x_high[lo:hi, :], x_low[lo:hi, :] = halves(part)
+    stores = [
+        pltpu.make_async_copy(factor, factor_hbm, out_sem.at[0]),
+        pltpu.make_async_copy(solved, solved_hbm, out_sem.at[1]),
+    ]
+    for store in stores:
+        store.start()
+    loads[4].wait()
+    for i in range(4):
+        a = slice(112 * i, 112 * i + 112)
+        trailing[a, :] = trailing[a, :] - thrice(d_high[a], d_low[a], x_high[:896, :], x_low[:896, :], NT)
+        store = pltpu.make_async_copy(trailing.at[a], updated_hbm.at[a], out_sem.at[2 + i])
+        store.start()
+        stores.append(store)
+    loads[5].wait()
+    rest[...] = rest[...] - thrice(x_high[896:1216, :], x_low[896:1216, :], d_high, d_low, NT)
+    store = pltpu.make_async_copy(rest, truth_hbm, out_sem.at[6])
+    store.start()
+    stores.append(store)
+    for store in stores:
+        store.wait()
+
+
+def apply_inverse(column, inverse, dealt, gathered, panel, trailing, rest):
+    f32, bf16 = jnp.float32, jnp.bfloat16
+    anywhere = pl.BlockSpec(memory_space=pl.ANY)
+    return pl.pallas_call(
+        apply_kernel,
+        out_shape=(
+            jax.ShapeDtypeStruct((28, 512), f32),
+            jax.ShapeDtypeStruct((448, 896), f32),
+            jax.ShapeDtypeStruct((16, 320), f32),
+            jax.ShapeDtypeStruct((320, 448), f32),
+        ),
+        in_specs=[pl.BlockSpec(memory_space=pltpu.SMEM)] + [anywhere] * 6,
+        out_specs=(anywhere,) * 4,
+        scratch_shapes=[
+            pltpu.VMEM((512, 512), f32),
+            pltpu.VMEM((16, 28, 512), f32),
+            pltpu.VMEM((32, 48, 512), f32),
+            pltpu.VMEM((28, 512), f32),
+            pltpu.VMEM((448, 896), f32),
+            pltpu.VMEM((320, 448), f32),
+            pltpu.VMEM((512, 512), bf16),
+            pltpu.VMEM((512, 512), bf16),
+            pltpu.VMEM((448, 512), f32),
+            pltpu.VMEM((1248, 512), f32),
+            pltpu.VMEM((1248, 512), bf16),
+            pltpu.VMEM((1248, 512), bf16),
+            pltpu.VMEM((28, 512), f32),
+            pltpu.VMEM((16, 320), f32),
+            pltpu.SemaphoreType.DMA((6,)),
+            pltpu.SemaphoreType.DMA((7,)),
+        ],
+        compiler_params=pltpu.CompilerParams(vmem_limit_bytes=48 * 2**20),
+        cost_estimate=pl.CostEstimate(flops=4 * 10**9, bytes_accessed=10**7, transcendentals=0),
+        name="apply_inverse",
+    )(column, inverse, dealt, gathered, panel, trailing, rest)
 
 
 def per_device(diag_block, panel, trailing, truth_panel, truth_rest):
@@ -111,19 +227,15 @@
     pieces = spread(diag_block.reshape(4, 128), columns, 32)
     strip = pieces.reshape(32, 4, 8, 16).transpose(1, 2, 0, 3).reshape(32, 512)
     whole = spread(strip, rows, 16).reshape(512, 512)
-    dealt = spread(panel, rows, 16).reshape(448, 512)
+    copies = jnp.broadcast_to(panel[None], (16, 28, 512))
+    copies, whole = lax.optimization_barrier((copies, whole))
+    dealt = lax.all_to_all(copies, rows, 0, 0)
     inverse = invert_factor(whole)
-    factor = lax.dot_general(panel, inverse, NT, precision=HI)
-    dealt_rows = lax.dot_general(dealt, inverse, NT, precision=HIGH)
-    own_rows = gathered[:, :28, :].reshape(896, 512)
-    factor_rows = lax.dot_general(own_rows, inverse, NT, precision=HIGH)
-    updated = trailing - lax.dot_general(factor_rows, dealt_rows, NT, precision=HIGH)
-    truth_rows = gathered[:, 32:, :320].reshape(512, 320)
-    solved_all = lax.dot_general(truth_rows, inverse, (((0,), (1,)), ((), ())), precision=HIGH)
-    at = (lax.axis_index("z") * 2 + lax.axis_index("k")) * 16
-    solved = lax.dynamic_slice_in_dim(solved_all, at, 16, 1)
-    truth_updated = truth_rest - lax.dot_general(solved_all, dealt_rows, NT, precision=HIGH)
-    return factor, updated, solved, truth_updated
+    column = (lax.axis_index("z") * 2 + lax.axis_index("k")).astype(jnp.int32)[None]
+    factor, updated, solved, truth_updated = apply_inverse(
+        column, inverse, dealt, gathered, panel, trailing.T, truth_rest
+    )
+    return factor, updated.T, solved.T, truth_updated
 
 
 def solution(mesh):

time: 142 us -> 116 us (0.82)
  matrix products: 16.2 us -> 0 us
  waiting for transfers between devices: 28.9 us -> 15 us
  Pallas kernels: 27.4 us -> 37.5 us
  local copies, waits for them, and re-layouts: 11.8 us -> 5.14 us
    dot_general x6 -> x0, matrix products: 16.2 us -> none  [the longest x1 4.21 us: per_device(): lax.dot_general(factor_rows, dealt_rows, NT, precision=HIGH)]
    all_to_all x2 -> x1, waiting for transfers between devices: 28.9 us -> 15 us  [spread(): return lax.all_to_all(copies, axes, 0, 0)]
    pallas_call x0 -> x1, Pallas kernels: none -> 10.2 us  [apply_inverse(): pl.pallas_call(apply_kernel, out_shape=(jax.ShapeDtypeStruct((28, 512), f...]
    all_to_all x0 -> x1, starting transfers between devices: none -> 4.31 us  [per_device(): dealt = lax.all_to_all(copies, rows, 0, 0)]
    all_to_all x2 -> x1, starting transfers between devices: 11.1 us -> 6.76 us  [spread(): return lax.all_to_all(copies, axes, 0, 0)]
    slice x2 -> x0, local copies, waits for them, and re-layouts: 3.9 us -> none  [the longest x1 2.1 us: per_device(): truth_rows = gathered[:, 32:, :320].reshape(512, 320)]
    broadcast_in_dim x5 -> x4, local copies, waits for them, and re-layouts: 3.4 us -> 1.46 us  [spread(): copies = jnp.broadcast_to(value[None], (count,) + value.shape)]
    reshape x2 -> x0, local copies, waits for them, and re-layouts: 1.55 us -> none  [the longest x1 1.45 us: per_device(): own_rows = gathered[:, :28, :].reshape(896, 512)]
  transfers between devices with their start and end apart: 3 -> 3, of which waited for: 2 -> 1; matrix products, arithmetic and copies ran while one was open for 7% -> 3% of each run, Pallas kernels for 19% -> 24%
where the time goes in v2:
time: 116 us; the launch traced here: 114 us
  Pallas kernels  37.5 us (32%)
  blocking collectives  29.6 us (26%)
  waiting for transfers between devices  15 us (13%)
  between operations  14.1 us (12%)
  starting transfers between devices  11.1 us (10%)
  local copies, waits for them, and re-layouts  5.14 us (4%)
  other arithmetic  1.51 us (1%)
    all_to_all x1, blocking collectives, spread(): return lax.all_to_all(copies, axes, 0, 0)  29.6 us
    pallas_call x1, Pallas kernels, invert_factor(): pl.pallas_call(chol_kernel, out_shape=jax.ShapeDtypeStruct((n, n), jnp.fl...  27.3 us
    all_to_all x1, waiting for transfers between devices, spread(): return lax.all_to_all(copies, axes, 0, 0)  15 us
    pallas_call x1, Pallas kernels, apply_inverse(): pl.pallas_call(apply_kernel, out_shape=(jax.ShapeDtypeStruct((28, 512), f...  10.2 us
    all_to_all x1, starting transfers between devices, spread(): return lax.all_to_all(copies, axes, 0, 0)  6.76 us
    all_to_all x1, starting transfers between devices, per_device(): dealt = lax.all_to_all(copies, rows, 0, 0)  4.31 us
  transfers between devices with their start and end apart: 3, of which 1 were waited for; matrix products, arithmetic and copies ran while one was open for 3% of the time, Pallas kernels for 24%

profile of v2, /device:TPU:1, one launch (start us, length us, event | category | flops | bytes accessed | tf_op | source)
XLA Modules:
  0.0 114.0 jit_solution(10392210335878920225)
XLA Ops:
  7.2 0.0 all-gather.3.cloned.1.call-start
  7.2 1.5 %select_maximum_fusion = f32[48,512]{1,0:T(8,128)} fusion(f32[16,320]{1,0:T(8,128)} %bitcast.15, f32[28,512]{1,0:T(8,128)} %panel_hbm.1), kind=kLoop, calls=%fused_computation | loop fusion | flops 122880 | bytes 176128 | tf_op jit(solution)/shard_map/concatenate | solution.py:219
  8.7 0.0 all-gather.3.cloned.1.call-update
  8.7 0.8 copy.11
  9.5 0.1 broadcast_in_dim.25
  9.6 29.6 %all_to_all.15 = f32[32,4,128]{2,1,0:T(4,128)S(1)} all-to-all(f32[32,4,128]{2,1,0:T(4,128)S(1)} %broadcast_in_dim.26), channel_id=1, replica_groups=mesh['x'=4,'y'=4,'z'=16,'k'=2] {'z','k'}, dimensions={0} | all-to-all | bytes 131072 | tf_op jit(solution)/shard_map/all_to_all | solution.py:95
  39.2 0.1 copy.12
  39.3 0.2 copy.13
  39.5 0.3 broadcast_in_dim.27
  39.8 1.1 broadcast_in_dim.28
  40.9 6.8 %all-to-all-start.1 = ((f32[16,32,512]{2,1,0:T(8,128)}), f32[16,32,512]{2,1,0:T(8,128)S(1)}, u32[]{:S(2)}, u32[]{:S(2)}) async-start(f32[16,32,512]{2,1,0:T(8,128)} %broadcast_in_dim.28), calls=%async_computation.1 | async-start | bytes 2097152 | tf_op jit(solution)/shard_map/all_to_all | solution.py:95
  47.7 15.0 %all-to-all-done.1 = f32[16,32,512]{2,1,0:T(8,128)S(1)} async-done(((f32[16,32,512]{2,1,0:T(8,128)}), f32[16,32,512]{2,1,0:T(8,128)S(1)}, u32[]{:S(2)}, u32[]{:S(2)}) %all-to-all-start.1) | async-done | bytes 1048608 | tf_op jit(solution)/shard_map/all_to_all | solution.py:95
  62.7 0.0 copy-done
  62.7 1.2 %broadcast_in_dim.24 = f32[16,28,512]{2,1,0:T(8,128)} broadcast(f32[28,512]{1,0:T(8,128)S(1)} %copy-done), dimensions={1,2} | broadcast | bytes 974848 | tf_op jit(solution)/shard_map/broadcast_in_dim | solution.py:230
  63.9 0.1 copy-done.4
  64.0 4.3 %all-to-all-start.2 = ((f32[16,28,512]{2,1,0:T(8,128)}), f32[16,28,512]{2,1,0:T(8,128)S(1)}, u32[]{:S(2)}, u32[]{:S(2)}) async-start(f32[16,28,512]{2,1,0:T(8,128)} %broadcast_in_dim.24), calls=%async_computation.2 | async-start | bytes 2097152 | tf_op jit(solution)/shard_map/all_to_all | solution.py:232
  68.3 0.0 copy-start.1
  68.3 0.0 copy-start.2
  68.4 27.3 %invert_factor.1.inv_hbm = f32[512,512]{1,0:T(8,128)} custom-call(f32[512,512]{1,0:T(8,128)} %bitcast.14), custom_call_target="tpu_custom_call" | custom-call | flops 10000000000 | bytes 2000000 | tf_op jit(solution)/shard_map/invert_factor/pallas_call | solution.py:77
  95.7 0.0 all-to-all-done.2.dealt_hbm
  95.7 0.0 copy-done.1
  95.7 0.0 copy-done.2
  95.7 1.2 %copy-done.3 = f32[512,512]{1,0:T(8,128)S(1)} copy-done((f32[512,512]{1,0:T(8,128)S(1)}, f32[512,512]{1,0:T(8,128)}, u32[]{:S(2)}) %copy-start.3) | copy-done | bytes 1048600
  96.9 10.2 %apply_inverse.1 = (f32[28,512]{1,0:T(8,128)}, f32[448,896]{1,0:T(8,128)}, f32[16,320]{1,0:T(8,128)}, f32[320,448]{1,0:T(8,128)}) custom-call(s32[1]{0:T(128)} %bitcast.col_ref, f32[512,512]{1,0:T(8,128)S(1)} %copy-done.3, f32[16,28,512]{2,1,0:T(8,128)S(1)} %all-to-all-done.2.dealt_hbm, f32[32,48,512]{2,1,0:T(8,128)} %bitcast.16, f32[28,512]{1,0:T(8,128)S(1)} %copy-done, ...), custom_call_target="tpu_custom_call" | custom-call | flops 4000000000 | bytes 10000000 | tf_op jit(solution)/shard_map/apply_inverse/pallas_call | solution.py:183
  (5 shorter events, 0.0 us)
Async XLA Ops:
  7.2 88.5 %all-gather.3.cloned.1.call-start = ((), (), s32[]{:S(2)}) async-start(), calls=%async_computation.3 | async-start | bytes 3244032 | tf_op jit(solution)/shard_map/all_gather | solution.py:226
  39.8 22.9 %copy-start = (f32[28,512]{1,0:T(8,128)S(1)}, f32[28,512]{1,0:T(8,128)}, u32[]{:S(2)}) copy-start(f32[28,512]{1,0:T(8,128)} %panel_hbm.1) | copy-start | bytes 172036
  40.9 21.8 %all-to-all-start.1 = ((f32[16,32,512]{2,1,0:T(8,128)}), f32[16,32,512]{2,1,0:T(8,128)S(1)}, u32[]{:S(2)}, u32[]{:S(2)}) async-start(f32[16,32,512]{2,1,0:T(8,128)} %broadcast_in_dim.28), calls=%async_computation.1 | async-start | bytes 2097152 | tf_op jit(solution)/shard_map/all_to_all | solution.py:95
  62.7 1.3 %copy-start.4 = (f32[16,32,512]{2,1,0:T(8,128)}, f32[16,32,512]{2,1,0:T(8,128)S(1)}, u32[]{:S(2)}) copy-start(f32[16,32,512]{2,1,0:T(8,128)S(1)} %all-to-all-done.1) | copy-start | bytes 3145732
  64.0 31.7 %all-to-all-start.2 = ((f32[16,28,512]{2,1,0:T(8,128)}), f32[16,28,512]{2,1,0:T(8,128)S(1)}, u32[]{:S(2)}, u32[]{:S(2)}) async-start(f32[16,28,512]{2,1,0:T(8,128)} %broadcast_in_dim.24), calls=%async_computation.2 | async-start | bytes 2097152 | tf_op jit(solution)/shard_map/all_to_all | solution.py:232
  68.3 27.3 %copy-start.1 = (f32[896,448]{0,1:T(8,128)S(1)}, f32[896,448]{0,1:T(8,128)}, u32[]{:S(2)}) copy-start(f32[896,448]{0,1:T(8,128)} %param.7) | copy-start | bytes 4816900
  68.3 27.3 %copy-start.2 = (f32[320,448]{1,0:T(8,128)S(1)}, f32[320,448]{1,0:T(8,128)}, u32[]{:S(2)}) copy-start(f32[320,448]{1,0:T(8,128)} %rest_hbm.1) | copy-start | bytes 1720324
  95.7 1.2 %copy-start.3 = (f32[512,512]{1,0:T(8,128)S(1)}, f32[512,512]{1,0:T(8,128)}, u32[]{:S(2)}) copy-start(f32[512,512]{1,0:T(8,128)} %invert_factor.1.inv_hbm) | copy-start | bytes 3145732
Sparse Core Ops, SparseCore 0:
  10.7 78.2 all-gather.2

commit v3 on v2

v3 whole, which is shorter than its diff:
```python
import jax
import jax.numpy as jnp
from jax import lax
from jax.experimental import pallas as pl
from jax.experimental.pallas import tpu as pltpu
from jax.sharding import PartitionSpec as P

HI = lax.Precision.HIGHEST
NT = (((1,), (1,)), ((), ()))
NN = (((1,), (0,)), ((), ()))


def halves(value):
    high = value.astype(jnp.bfloat16)
    return high, (value - high.astype(jnp.float32)).astype(jnp.bfloat16)


def factor_tile(d_ref, o_ref):
    n = 16
    lane = lax.broadcasted_iota(jnp.int32, (8, 128), 1)
    sub = lax.broadcasted_iota(jnp.int32, (8, 128), 0)
    full = lambda v: jnp.broadcast_to(v, (8, 128))
    m = [d_ref[8 * i:8 * i + 8, :] for i in range(n)]
    own = [full(m[0][:, c:c + 1]) for c in range(8)]
    for j in range(n):
        lo = 8 * j
        here = (lane >= lo) & (lane < lo + 8)
        s = {(a, c): full(own[c][a:a + 1, :]) for c in range(8) for a in range(c, 8)}
        rows = jnp.where(here, jnp.where(lane - lo == sub, 1.0, 0.0), m[j])
        r = [full(rows[a:a + 1, :]) for a in range(8)]
        if j + 1 < n:
            raw = [full(m[j + 1][:, lo + c:lo + c + 1]) for c in range(8)]
            own = [full(m[j + 1][:, lo + 8 + c:lo + 9 + c]) for c in range(8)]
            t = list(raw)
            near = jnp.where(here, 0.0, m[j + 1])
        l, inv, u = {}, [], []
        for c in range(8):
            q = lax.rsqrt(s[c, c])
            inv.append(q)
            for a in range(c + 1, 8):
                l[a, c] = s[a, c] * q
            for a in range(c + 1, 8):
                for b in range(c + 1, a + 1):
                    s[a, b] = s[a, b] - l[a, c] * l[b, c]
            u.append(r[c] * q)
            for a in range(c + 1, 8):
                r[a] = r[a] - l[a, c] * u[c]
            if j + 1 < n:
                t[c] = t[c] * q
                for a in range(c + 1, 8):
                    t[a] = t[a] - t[c] * l[a, c]
                for a in range(8):
                    own[a] = own[a] - t[c] * full(t[c][a:a + 1, :])
                near = near - t[c] * u[c]
        done = u[0]
        for a in range(1, 8):
            done = jnp.where(sub == a, u[a], done)
        o_ref[lo:lo + 8, :] = jnp.where(lane < lo + 8, done, 0.0)
        if j + 1 < n:
            m[j + 1] = near
        if j + 2 < n:
            v = [None] * 8
            for c in range(7, -1, -1):
                x = u[c]
                for a in range(7, c, -1):
                    x = x - l[a, c] * v[a]
                v[c] = x * inv[c]
            for i in range(j + 2, n):
                acc = jnp.where(here, 0.0, m[i])
                for c in range(8):
                    acc = acc - full(m[i][:, lo + c:lo + c + 1]) * v[c]
                m[i] = acc


def invert_kernel(a_hbm, high_hbm, low_hbm, m_ref, d_ref, t_ref, o_ref, high_ref, low_ref, sem):
    nb, n = 128, 512
    load = pltpu.make_async_copy(a_hbm, m_ref, sem.at[0])
    load.start()
    load.wait()
    dot = lambda p, q, dims: lax.dot_general(p, q, dims, precision=HI, preferred_element_type=jnp.float32)

    def after(k):
        lo, hi = k * nb, (k + 1) * nb
        t = t_ref[...]
        o_ref[lo:hi, lo:hi] = t
        if lo:
            o_ref[lo:hi, :lo] = dot(t, m_ref[lo:hi, :lo], NN)
        if hi < n:
            o_ref[lo:hi, hi:] = jnp.zeros((nb, n - hi), jnp.float32)
            left = dot(m_ref[hi:, lo:hi], t, NT)
            m_ref[hi:, hi:] = m_ref[hi:, hi:] - dot(left, left, NT)
            m_ref[hi:, lo:hi] = -dot(left, t, NN)
            if lo:
                m_ref[hi:, :lo] = m_ref[hi:, :lo] - dot(left, o_ref[lo:hi, :lo], NN)

    def step(k, carry):
        at = pl.ds(pl.multiple_of(k * nb, nb), nb)
        d_ref[...] = m_ref[at, at]
        factor_tile(d_ref, t_ref)
        for i in range(n // nb):
            pl.when(k == i)(lambda i=i: after(i))
        return carry

    lax.fori_loop(0, n // nb, step, 0)
    high_ref[...], low_ref[...] = halves(o_ref[...])
    stores = [
        pltpu.make_async_copy(high_ref, high_hbm, sem.at[1]),
        pltpu.make_async_copy(low_ref, low_hbm, sem.at[2]),
    ]
    for store in stores:
        store.start()
    for store in stores:
        store.wait()


def invert_factor(block):
    n = block.shape[0]
    anywhere = pl.BlockSpec(memory_space=pl.ANY)
    half = jax.ShapeDtypeStruct((n, n), jnp.bfloat16)
    return pl.pallas_call(
        invert_kernel,
        out_shape=(half, half),
        in_specs=[anywhere],
        out_specs=(anywhere, anywhere),
        scratch_shapes=[
            pltpu.VMEM((n, n), jnp.float32),
            pltpu.VMEM((128, 128), jnp.float32),
            pltpu.VMEM((128, 128), jnp.float32),
            pltpu.VMEM((n, n), jnp.float32),
            pltpu.VMEM((n, n), jnp.bfloat16),
            pltpu.VMEM((n, n), jnp.bfloat16),
            pltpu.SemaphoreType.DMA((3,)),
        ],
        compiler_params=pltpu.CompilerParams(vmem_limit_bytes=16 * 2**20),
        cost_estimate=pl.CostEstimate(flops=10**10, bytes_accessed=2 * 10**6, transcendentals=0),
        name="invert_factor",
    )(block)


def spread(value, axes, count):
    copies = jnp.broadcast_to(value[None], (count,) + value.shape)
    return lax.all_to_all(copies, axes, 0, 0)


def thrice(a_high, a_low, b_high, b_low, dims):
    dot = lambda p, q: lax.dot_general(p, q, dims, preferred_element_type=jnp.float32)
    return dot(a_high, b_high) + dot(a_high, b_low) + dot(a_low, b_high)


def apply_kernel(
    col_ref, high_hbm, low_hbm, dealt_hbm, gathered_hbm, panel_hbm, trailing_hbm, rest_hbm,
    factor_hbm, updated_hbm, solved_hbm, truth_hbm,
    inv_high, inv_low, dealt, gathered, panel, trailing, rest,
    row_high, row_low, x_high, x_low, factor, solved, sem, out_sem,
):
    loads = [
        pltpu.make_async_copy(src, dst, sem.at[i])
        for i, (src, dst) in enumerate(
            [
                (high_hbm, inv_high), (low_hbm, inv_low), (dealt_hbm, dealt), (gathered_hbm, gathered),
                (panel_hbm, panel), (trailing_hbm, trailing), (rest_hbm, rest),
            ]
        )
    ]
    for load in loads:
        load.start()
    loads[0].wait()
    loads[1].wait()

    def solve(high, low):
        a = thrice(high[:, :256], low[:, :256], inv_high[:256, :256], inv_low[:256, :256], NT)
        b = thrice(high, low, inv_high[256:, :], inv_low[256:, :], NT)
        return jnp.concatenate([a, b], 1)

    loads[2].wait()
    for r in range(16):
        row_high[28 * r:28 * r + 28, :] = dealt[r]
    high, low = halves(row_high[...])
    done = solve(high, low)
    d_high, d_low = halves(done)
    loads[3].wait()
    loads[4].wait()
    stack = row_low
    for c in range(32):
        stack[28 * c:28 * c + 28, :] = gathered[c, 0:28, :]
    truth = gathered[:, 32:48, 0:384].reshape(512, 384)
    stack[896:1216, :] = truth.T[0:320, :]
    stack[1216:1244, :] = panel[...]
    stack[1244:1248, :] = jnp.zeros((4, 512), jnp.float32)
    at = pl.ds(pl.multiple_of(col_ref[0] * 16, 16), 16)
    i_high, i_low = inv_high[at, :], inv_low[at, :]
    t_high, t_low = halves(stack[896:1216, :])
    solved[...] = thrice(i_high, i_low, t_high, t_low, NT)
    for lo, hi in ((0, 416), (416, 832), (832, 1248)):
        high, low = halves(stack[lo:hi, :])
        part = solve(high, low)
        if hi == 1248:
            factor[...] = part[1216 - lo:1244 - lo, :]
        x_high[lo:hi, :], x_low[lo:hi, :] = halves(part)
    stores = [
        pltpu.make_async_copy(factor, factor_hbm, out_sem.at[0]),
        pltpu.make_async_copy(solved, solved_hbm, out_sem.at[1]),
    ]
    for store in stores:
        store.start()
    loads[5].wait()
    for i in range(4):
        a = slice(112 * i, 112 * i + 112)
        trailing[a, :] = trailing[a, :] - thrice(d_high[a], d_low[a], x_high[:896, :], x_low[:896, :], NT)
        store = pltpu.make_async_copy(trailing.at[a], updated_hbm.at[a], out_sem.at[2 + i])
        store.start()
        stores.append(store)
    loads[6].wait()
    rest[...] = rest[...] - thrice(x_high[896:1216, :], x_low[896:1216, :], d_high, d_low, NT)
    store = pltpu.make_async_copy(rest, truth_hbm, out_sem.at[6])
    store.start()
    stores.append(store)
    for store in stores:
        store.wait()


def apply_inverse(column, high, low, dealt, gathered, panel, trailing, rest):
    f32, bf16 = jnp.float32, jnp.bfloat16
    anywhere = pl.BlockSpec(memory_space=pl.ANY)
    keep = pltpu.with_memory_space_constraint
    return pl.pallas_call(
        apply_kernel,
        out_shape=(
            jax.ShapeDtypeStruct((28, 512), f32),
            jax.ShapeDtypeStruct((448, 896), f32),
            jax.ShapeDtypeStruct((16, 320), f32),
            jax.ShapeDtypeStruct((320, 448), f32),
        ),
        in_specs=[pl.BlockSpec(memory_space=pltpu.SMEM)] + [anywhere] * 3 + [pl.BlockSpec(memory_space=pltpu.HBM)] * 4,
        out_specs=(pl.BlockSpec(memory_space=pltpu.HBM),) * 4,
        scratch_shapes=[
            pltpu.VMEM((512, 512), bf16),
            pltpu.VMEM((512, 512), bf16),
            pltpu.VMEM((16, 28, 512), f32),
            pltpu.VMEM((32, 48, 512), f32),
            pltpu.VMEM((28, 512), f32),
            pltpu.VMEM((448, 896), f32),
            pltpu.VMEM((320, 448), f32),
            pltpu.VMEM((448, 512), f32),
            pltpu.VMEM((1248, 512), f32),
            pltpu.VMEM((1248, 512), bf16),
            pltpu.VMEM((1248, 512), bf16),
            pltpu.VMEM((28, 512), f32),
            pltpu.VMEM((16, 320), f32),
            pltpu.SemaphoreType.DMA((7,)),
            pltpu.SemaphoreType.DMA((7,)),
        ],
        compiler_params=pltpu.CompilerParams(vmem_limit_bytes=24 * 2**20),
        cost_estimate=pl.CostEstimate(flops=4 * 10**9, bytes_accessed=10**7, transcendentals=0),
        name="apply_inverse",
    )(column, high, low, dealt, *(keep(x, pltpu.HBM) for x in (gathered, panel, trailing, rest)))


def per_device(diag_block, panel, trailing, truth_panel, truth_rest):
    rows, columns = ("x", "y"), ("z", "k")
    packed = jnp.concatenate(
        [
            jnp.pad(panel, ((0, 4), (0, 0))),
            jnp.pad(truth_panel.T, ((0, 0), (0, 192))),
        ],
        0,
    )
    gathered = lax.all_gather(packed, columns, axis=0, tiled=False)
    pieces = spread(diag_block.reshape(4, 128), columns, 32)
    strip = pieces.reshape(32, 4, 8, 16).transpose(1, 2, 0, 3).reshape(32, 512)
    whole = spread(strip, rows, 16).reshape(512, 512)
    copies = jnp.broadcast_to(panel[None], (16, 28, 512))
    copies, whole = lax.optimization_barrier((copies, whole))
    dealt = lax.all_to_all(copies, rows, 0, 0)
    high, low = invert_factor(whole)
    column = (lax.axis_index("z") * 2 + lax.axis_index("k")).astype(jnp.int32)[None]
    factor, updated, solved, truth_updated = apply_inverse(
        column, high, low, dealt, gathered, panel, trailing.T, truth_rest
    )
    return factor, updated.T, solved.T, truth_updated


def solution(mesh):
    fine = jax.sharding.Mesh(mesh.devices.reshape(4, 4, 16, 2), ("x", "y", "z", "k"))
    rows, columns = ("x", "y"), ("z", "k")
    tiled, whole = P(rows, columns), P(rows + columns, None)
    return jax.shard_map(
        per_device,
        mesh=fine,
        in_specs=(tiled, whole, tiled, tiled, tiled),
        out_specs=(whole, tiled, tiled, tiled),
        check_vma=False,
    )
```

time: 116 us -> 106 us (0.914); the launches traced: 114 us -> 106 us
  Pallas kernels: 37.5 us -> 23.8 us
  waiting for transfers between devices: 15 us -> 22.3 us
  local copies, waits for them, and re-layouts: 5.14 us -> 3.7 us
    pallas_call x1, Pallas kernels: 27.3 us -> 13.6 us  [invert_factor(): pl.pallas_call(invert_kernel, out_shape=(half, half), in_specs=[anywhere]...]
    all_gather x1, waiting for transfers between devices: 0.01 us -> 6.25 us  [per_device(): gathered = lax.all_gather(packed, columns, axis=0, tiled=False)]
    unnamed x11 -> x3, local copies, waits for them, and re-layouts: 2.11 us -> 0.78 us
  transfers between devices with their start and end apart: 3 -> 3, of which waited for: 1 -> 3; matrix products, arithmetic and copies ran while one was open for 3% -> 3% of each run, Pallas kernels for 24% -> 13%
where the time goes in v3:
time: 106 us
  blocking collectives  29.6 us (28%)
  Pallas kernels  23.8 us (22%)
  waiting for transfers between devices  22.3 us (21%)
  between operations  14.1 us (13%)
  starting transfers between devices  11.1 us (10%)
  local copies, waits for them, and re-layouts  3.7 us (3%)
  other arithmetic  1.51 us (1%)
    all_to_all x1, blocking collectives, spread(): return lax.all_to_all(copies, axes, 0, 0)  29.6 us
    all_to_all x1, waiting for transfers between devices, spread(): return lax.all_to_all(copies, axes, 0, 0)  15 us
    pallas_call x1, Pallas kernels, invert_factor(): pl.pallas_call(invert_kernel, out_shape=(half, half), in_specs=[anywhere]...  13.6 us
    pallas_call x1, Pallas kernels, apply_inverse(): pl.pallas_call(apply_kernel, out_shape=(jax.ShapeDtypeStruct((28, 512), f...  10.2 us
    all_to_all x1, starting transfers between devices, spread(): return lax.all_to_all(copies, axes, 0, 0)  6.76 us
    all_gather x1, waiting for transfers between devices, per_device(): gathered = lax.all_gather(packed, columns, axis=0, tiled=False)  6.25 us
    all_to_all x1, starting transfers between devices, per_device(): dealt = lax.all_to_all(copies, rows, 0, 0)  4.31 us
  transfers between devices with their start and end apart: 3, of which 3 were waited for; matrix products, arithmetic and copies ran while one was open for 3% of the time, Pallas kernels for 13%

profile of v3, /device:TPU:1, one launch (start us, length us, event | category | flops | bytes accessed | tf_op | source)
XLA Modules:
  0.0 106.0 jit_solution(12692675418420286178)
XLA Ops:
  7.2 0.0 all-gather.3.cloned.1.call-start
  7.2 1.5 %select_maximum_fusion = f32[48,512]{1,0:T(8,128)} fusion(f32[16,320]{1,0:T(8,128)} %bitcast.14, f32[28,512]{1,0:T(8,128)} %panel_hbm.1), kind=kLoop, calls=%fused_computation | loop fusion | flops 122880 | bytes 176128 | tf_op jit(solution)/shard_map/concatenate | solution.py:261
  8.7 0.0 all-gather.3.cloned.1.call-update
  8.7 0.8 copy.11
  9.5 0.1 broadcast_in_dim.25
  9.6 29.6 %all_to_all.15 = f32[32,4,128]{2,1,0:T(4,128)S(1)} all-to-all(f32[32,4,128]{2,1,0:T(4,128)S(1)} %broadcast_in_dim.26), channel_id=1, replica_groups=mesh['x'=4,'y'=4,'z'=16,'k'=2] {'z','k'}, dimensions={0} | all-to-all | bytes 131072 | tf_op jit(solution)/shard_map/all_to_all | solution.py:142
  39.2 0.1 copy.12
  39.3 0.2 copy.13
  39.5 0.3 broadcast_in_dim.27
  39.8 0.0 copy-start
  39.8 1.1 %broadcast_in_dim.28 = f32[16,32,512]{2,1,0:T(8,128)} broadcast(f32[32,512]{1,0:T(8,128)S(1)} %broadcast_in_dim.27), dimensions={1,2} | broadcast | bytes 1114112 | tf_op jit(solution)/shard_map/broadcast_in_dim | solution.py:141
  40.9 6.8 %all-to-all-start.1 = ((f32[16,32,512]{2,1,0:T(8,128)}), f32[16,32,512]{2,1,0:T(8,128)S(1)}, u32[]{:S(2)}, u32[]{:S(2)}) async-start(f32[16,32,512]{2,1,0:T(8,128)} %broadcast_in_dim.28), calls=%async_computation.1 | async-start | bytes 2097152 | tf_op jit(solution)/shard_map/all_to_all | solution.py:142
  47.7 15.0 %all-to-all-done.1 = f32[16,32,512]{2,1,0:T(8,128)S(1)} async-done(((f32[16,32,512]{2,1,0:T(8,128)}), f32[16,32,512]{2,1,0:T(8,128)S(1)}, u32[]{:S(2)}, u32[]{:S(2)}) %all-to-all-start.1) | async-done | bytes 1048608 | tf_op jit(solution)/shard_map/all_to_all | solution.py:142
  62.7 0.0 copy-done
  62.7 1.1 %broadcast_in_dim.24 = f32[16,28,512]{2,1,0:T(8,128)} broadcast(f32[28,512]{1,0:T(8,128)S(1)} %copy-done), dimensions={1,2} | broadcast | bytes 974848 | tf_op jit(solution)/shard_map/broadcast_in_dim | solution.py:272
  63.8 4.3 %all-to-all-start.2 = ((f32[16,28,512]{2,1,0:T(8,128)}), f32[16,28,512]{2,1,0:T(8,128)S(1)}, u32[]{:S(2)}, u32[]{:S(2)}) async-start(f32[16,28,512]{2,1,0:T(8,128)} %broadcast_in_dim.24), calls=%async_computation.2 | async-start | bytes 2097152 | tf_op jit(solution)/shard_map/all_to_all | solution.py:274
  68.1 13.6 %invert_factor.1 = (bf16[512,512]{1,0:T(8,128)(2,1)S(1)}, bf16[512,512]{1,0:T(8,128)(2,1)S(1)}) custom-call(f32[512,512]{1,0:T(8,128)S(1)} %bitcast.12), custom_call_target="tpu_custom_call" | custom-call | flops 10000000000 | bytes 2000000 | tf_op jit(solution)/shard_map/invert_factor/pallas_call | solution.py:120
  81.7 1.0 all-to-all-done.2.dealt_hbm
  82.7 6.3 %all-gather.3.cloned.1.call-done = f32[1536,512]{1,0:T(8,128)} async-done(((f32[48,512]{1,0:T(8,128)}), f32[1536,512]{1,0:T(8,128)}) %all-gather.3.cloned.1.call-update) | async-done | bytes 3145744 | tf_op jit(solution)/shard_map/all_gather | solution.py:268
  89.0 10.2 %apply_inverse.1 = (f32[28,512]{1,0:T(8,128)}, f32[448,896]{1,0:T(8,128)}, f32[16,320]{1,0:T(8,128)}, f32[320,448]{1,0:T(8,128)}) custom-call(s32[1]{0:T(128)} %bitcast.col_ref, bf16[512,512]{1,0:T(8,128)(2,1)S(1)} %get-tuple-element.13.high_hbm, bf16[512,512]{1,0:T(8,128)(2,1)S(1)} %get-tuple-element.14.low_hbm, ...), custom_call_target="tpu_custom_call" | custom-call | flops 4000000000 | bytes 10000000 | tf_op jit(solution)/shard_map/apply_inverse/pallas_call | solution.py:226
  (1 shorter events, 0.0 us)
Async XLA Ops:
  7.2 81.8 %all-gather.3.cloned.1.call-start = ((), (), s32[]{:S(2)}) async-start(), calls=%async_computation.3 | async-start | bytes 3244032 | tf_op jit(solution)/shard_map/all_gather | solution.py:268
  39.8 22.9 %copy-start = (f32[28,512]{1,0:T(8,128)S(1)}, f32[28,512]{1,0:T(8,128)}, u32[]{:S(2)}) copy-start(f32[28,512]{1,0:T(8,128)} %panel_hbm.1) | copy-start | bytes 172036
  40.9 21.8 %all-to-all-start.1 = ((f32[16,32,512]{2,1,0:T(8,128)}), f32[16,32,512]{2,1,0:T(8,128)S(1)}, u32[]{:S(2)}, u32[]{:S(2)}) async-start(f32[16,32,512]{2,1,0:T(8,128)} %broadcast_in_dim.28), calls=%async_computation.1 | async-start | bytes 2097152 | tf_op jit(solution)/shard_map/all_to_all | solution.py:142
  63.8 18.9 %all-to-all-start.2 = ((f32[16,28,512]{2,1,0:T(8,128)}), f32[16,28,512]{2,1,0:T(8,128)S(1)}, u32[]{:S(2)}, u32[]{:S(2)}) async-start(f32[16,28,512]{2,1,0:T(8,128)} %broadcast_in_dim.24), calls=%async_computation.2 | async-start | bytes 2097152 | tf_op jit(solution)/shard_map/all_to_all | solution.py:274
Sparse Core Ops, SparseCore 0:
  10.7 78.2 all-gather.2

commit v4 on v3

--- a/solution.py
+++ b/solution.py
@@ -137,9 +137,52 @@
     )(block)
 
 
-def spread(value, axes, count):
-    copies = jnp.broadcast_to(value[None], (count,) + value.shape)
-    return lax.all_to_all(copies, axes, 0, 0)
+def pack_kernel(panel_ref, truth_ref, packed_ref, copies_hbm, sem):
+    copies = [pltpu.make_async_copy(panel_ref, copies_hbm.at[i], sem.at[i]) for i in range(16)]
+    for copy in copies:
+        copy.start()
+    packed_ref[0:8, 0:256] = truth_ref[0:8, 0:256]
+    packed_ref[0:8, 256:512] = truth_ref[8:16, 0:256]
+    packed_ref[8:12, :] = jnp.zeros((4, 512), jnp.float32)
+    for q in range(4):
+        packed_ref[8:12, 128 * q:128 * q + 64] = truth_ref[4 * q:4 * q + 4, 256:320]
+    packed_ref[12:40, :] = panel_ref[...]
+    for copy in copies:
+        copy.wait()
+
+
+def pack(panel, truth):
+    f32 = jnp.float32
+    whole = pl.BlockSpec(memory_space=pltpu.VMEM)
+    return pl.pallas_call(
+        pack_kernel,
+        out_shape=(jax.ShapeDtypeStruct((40, 512), f32), jax.ShapeDtypeStruct((16, 28, 512), f32)),
+        in_specs=[whole, whole],
+        out_specs=(whole, pl.BlockSpec(memory_space=pl.ANY)),
+        scratch_shapes=[pltpu.SemaphoreType.DMA((16,))],
+        compiler_params=pltpu.CompilerParams(vmem_limit_bytes=4 * 2**20),
+        name="pack",
+    )(panel, truth)
+
+
+def copy_kernel(strip_ref, copies_hbm, sem):
+    copies = [pltpu.make_async_copy(strip_ref, copies_hbm.at[i], sem.at[i]) for i in range(16)]
+    for copy in copies:
+        copy.start()
+    for copy in copies:
+        copy.wait()
+
+
+def copy_out(strip):
+    return pl.pallas_call(
+        copy_kernel,
+        out_shape=jax.ShapeDtypeStruct((16,) + strip.shape, strip.dtype),
+        in_specs=[pl.BlockSpec(memory_space=pltpu.VMEM)],
+        out_specs=pl.BlockSpec(memory_space=pl.ANY),
+        scratch_shapes=[pltpu.SemaphoreType.DMA((16,))],
+        compiler_params=pltpu.CompilerParams(vmem_limit_bytes=4 * 2**20),
+        name="copy_out",
+    )(strip)
 
 
 def thrice(a_high, a_low, b_high, b_low, dims):
@@ -151,7 +194,7 @@
     col_ref, high_hbm, low_hbm, dealt_hbm, gathered_hbm, panel_hbm, trailing_hbm, rest_hbm,
     factor_hbm, updated_hbm, solved_hbm, truth_hbm,
     inv_high, inv_low, dealt, gathered, panel, trailing, rest,
-    row_high, row_low, x_high, x_low, factor, solved, sem, out_sem,
+    row_high, row_low, truth, x_high, x_low, factor, solved, sem, out_sem,
 ):
     loads = [
         pltpu.make_async_copy(src, dst, sem.at[i])
@@ -182,9 +225,12 @@
     loads[4].wait()
     stack = row_low
     for c in range(32):
-        stack[28 * c:28 * c + 28, :] = gathered[c, 0:28, :]
-    truth = gathered[:, 32:48, 0:384].reshape(512, 384)
-    stack[896:1216, :] = truth.T[0:320, :]
+        stack[28 * c:28 * c + 28, :] = gathered[c, 12:40, :]
+        truth[16 * c:16 * c + 8, 0:256] = gathered[c, 0:8, 0:256]
+        truth[16 * c + 8:16 * c + 16, 0:256] = gathered[c, 0:8, 256:512]
+        for q in range(4):
+            truth[16 * c + 4 * q:16 * c + 4 * q + 4, 256:384] = gathered[c, 8:12, 128 * q:128 * q + 128]
+    stack[896:1216, :] = truth[...].T[0:320, :]
     stack[1216:1244, :] = panel[...]
     stack[1244:1248, :] = jnp.zeros((4, 512), jnp.float32)
     at = pl.ds(pl.multiple_of(col_ref[0] * 16, 16), 16)
@@ -237,12 +283,13 @@
             pltpu.VMEM((512, 512), bf16),
             pltpu.VMEM((512, 512), bf16),
             pltpu.VMEM((16, 28, 512), f32),
-            pltpu.VMEM((32, 48, 512), f32),
+            pltpu.VMEM((32, 40, 512), f32),
             pltpu.VMEM((28, 512), f32),
             pltpu.VMEM((448, 896), f32),
             pltpu.VMEM((320, 448), f32),
             pltpu.VMEM((448, 512), f32),
             pltpu.VMEM((1248, 512), f32),
+            pltpu.VMEM((512, 384), f32),
             pltpu.VMEM((1248, 512), bf16),
             pltpu.VMEM((1248, 512), bf16),
             pltpu.VMEM((28, 512), f32),
@@ -258,18 +305,12 @@
 
 def per_device(diag_block, panel, trailing, truth_panel, truth_rest):
     rows, columns = ("x", "y"), ("z", "k")
-    packed = jnp.concatenate(
-        [
-            jnp.pad(panel, ((0, 4), (0, 0))),
-            jnp.pad(truth_panel.T, ((0, 0), (0, 192))),
-        ],
-        0,
-    )
+    packed, copies = pack(panel, truth_panel.T)
     gathered = lax.all_gather(packed, columns, axis=0, tiled=False)
-    pieces = spread(diag_block.reshape(4, 128), columns, 32)
+    small = jnp.broadcast_to(diag_block.reshape(1, 4, 128), (32, 4, 128))
+    pieces = lax.all_to_all(small, columns, 0, 0)
     strip = pieces.reshape(32, 4, 8, 16).transpose(1, 2, 0, 3).reshape(32, 512)
-    whole = spread(strip, rows, 16).reshape(512, 512)
-    copies = jnp.broadcast_to(panel[None], (16, 28, 512))
+    whole = lax.all_to_all(copy_out(strip), rows, 0, 0).reshape(512, 512)
     copies, whole = lax.optimization_barrier((copies, whole))
     dealt = lax.all_to_all(copies, rows, 0, 0)
     high, low = invert_factor(whole)

time: 106 us -> 106 us (level)
  Pallas kernels: 23.8 us -> 26.5 us
  other arithmetic: 1.51 us -> 0 us
    pallas_call x0 -> x2, Pallas kernels: none -> 2.87 us  [the longest x1 1.77 us: pack(): pl.pallas_call(pack_kernel, out_shape=(jax.ShapeDtypeStruct((40, 512), f3...]
    broadcast_in_dim x5 -> x2, local copies, waits for them, and re-layouts: 2.56 us -> 0.09 us  [per_device(): small = jnp.broadcast_to(diag_block.reshape(1, 4, 128), (32, 4, 128))]
    unnamed x3 -> x5, local copies, waits for them, and re-layouts: 0.78 us -> 2.34 us
    concatenate x1 -> x0, other arithmetic: 1.51 us -> none  [per_device(): jnp.concatenate([jnp.pad(panel, ((0, 4), (0, 0))), jnp.pad(truth_panel.T,...]
    all_gather x1, waiting for transfers between devices: 6.25 us -> 5.14 us  [per_device(): gathered = lax.all_gather(packed, columns, axis=0, tiled=False)]
  transfers between devices with their start and end apart: 3 -> 3, of which waited for: 3 -> 3; matrix products, arithmetic and copies ran while one was open for 3% -> 1% of each run, Pallas kernels for 13% -> 14%
where the time goes in v4:
time: 106 us; the launch traced here: 105 us
  blocking collectives  29.6 us (28%)
  Pallas kernels  26.5 us (25%)
  waiting for transfers between devices  21.3 us (20%)
  between operations  14.1 us (13%)
  starting transfers between devices  10.9 us (10%)
  local copies, waits for them, and re-layouts  3.06 us (3%)
    all_to_all x1, blocking collectives, per_device(): pieces = lax.all_to_all(small, columns, 0, 0)  29.6 us
    all_to_all x1, waiting for transfers between devices, per_device(): whole = lax.all_to_all(copy_out(strip), rows, 0, 0).reshape(512, 512)  15.1 us
    pallas_call x1, Pallas kernels, invert_factor(): pl.pallas_call(invert_kernel, out_shape=(half, half), in_specs=[anywhere]...  13.6 us
    pallas_call x1, Pallas kernels, apply_inverse(): pl.pallas_call(apply_kernel, out_shape=(jax.ShapeDtypeStruct((28, 512), f...  10.1 us
    all_to_all x1, starting transfers between devices, per_device(): whole = lax.all_to_all(copy_out(strip), rows, 0, 0).reshape(512, 512)  6.77 us
    all_gather x1, waiting for transfers between devices, per_device(): gathered = lax.all_gather(packed, columns, axis=0, tiled=False)  5.14 us
    all_to_all x1, starting transfers between devices, per_device(): dealt = lax.all_to_all(copies, rows, 0, 0)  4.11 us
    unnamed x5, local copies, waits for them, and re-layouts  2.34 us
  transfers between devices with their start and end apart: 3, of which 3 were waited for; matrix products, arithmetic and copies ran while one was open for 1% of the time, Pallas kernels for 14%

profile of v4, /device:TPU:1, one launch (start us, length us, event | category | flops | bytes accessed | tf_op | source)
XLA Modules:
  0.0 105.5 jit_solution(207848657686057241)
XLA Ops:
  7.2 0.0 all-gather.3.cloned.1.call-start
  7.2 0.0 copy-start
  7.2 0.8 copy-done
  8.1 0.0 copy-start.1
  8.1 0.7 copy-done.1
  8.8 1.8 %pack.1 = (f32[40,512]{1,0:T(8,128)}, f32[16,28,512]{2,1,0:T(8,128)}) custom-call(f32[28,512]{1,0:T(8,128)S(1)} %copy-done, f32[16,320]{1,0:T(8,128)S(1)} %bitcast.13), custom_call_target="tpu_custom_call" | custom-call | tf_op jit(solution)/shard_map/pack/pallas_call | solution.py:157
  10.6 0.0 all-gather.3.cloned.1.call-update
  10.6 0.8 copy.11
  11.4 0.1 broadcast_in_dim.11
  11.5 29.6 %all_to_all.15 = f32[32,4,128]{2,1,0:T(4,128)S(1)} all-to-all(f32[32,4,128]{2,1,0:T(4,128)S(1)} %broadcast_in_dim.12), channel_id=1, replica_groups=mesh['x'=4,'y'=4,'z'=16,'k'=2] {'z','k'}, dimensions={0} | all-to-all | bytes 131072 | tf_op jit(solution)/shard_map/all_to_all | solution.py:311
  41.0 0.1 copy.12
  41.2 0.2 copy.13
  41.4 0.3 reshape.20.strip_ref
  41.7 1.1 %copy_out.1 = f32[16,32,512]{2,1,0:T(8,128)} custom-call(f32[32,512]{1,0:T(8,128)S(1)} %reshape.20.strip_ref), custom_call_target="tpu_custom_call" | custom-call | tf_op jit(solution)/shard_map/copy_out/pallas_call | solution.py:177
  42.8 6.8 %all-to-all-start.1 = ((f32[16,32,512]{2,1,0:T(8,128)}), f32[16,32,512]{2,1,0:T(8,128)S(1)}, u32[]{:S(2)}, u32[]{:S(2)}) async-start(f32[16,32,512]{2,1,0:T(8,128)} %copy_out.1), calls=%async_computation.1 | async-start | bytes 2097152 | tf_op jit(solution)/shard_map/all_to_all | solution.py:313
  49.5 15.1 %all-to-all-done.1 = f32[16,32,512]{2,1,0:T(8,128)S(1)} async-done(((f32[16,32,512]{2,1,0:T(8,128)}), f32[16,32,512]{2,1,0:T(8,128)S(1)}, u32[]{:S(2)}, u32[]{:S(2)}) %all-to-all-start.1) | async-done | bytes 1048608 | tf_op jit(solution)/shard_map/all_to_all | solution.py:313
  64.7 4.1 %all-to-all-start.2 = ((f32[16,28,512]{2,1,0:T(8,128)}), f32[16,28,512]{2,1,0:T(8,128)S(1)}, u32[]{:S(2)}, u32[]{:S(2)}) async-start(f32[16,28,512]{2,1,0:T(8,128)} %get-tuple-element.18), calls=%async_computation.2 | async-start | bytes 2097152 | tf_op jit(solution)/shard_map/all_to_all | solution.py:315
  68.8 13.6 %invert_factor.1 = (bf16[512,512]{1,0:T(8,128)(2,1)S(1)}, bf16[512,512]{1,0:T(8,128)(2,1)S(1)}) custom-call(f32[512,512]{1,0:T(8,128)S(1)} %bitcast.12), custom_call_target="tpu_custom_call" | custom-call | flops 10000000000 | bytes 2000000 | tf_op jit(solution)/shard_map/invert_factor/pallas_call | solution.py:120
  82.4 1.1 all-to-all-done.2.dealt_hbm
  83.4 5.1 %all-gather.3.cloned.1.call-done = f32[1280,512]{1,0:T(8,128)} async-done(((f32[40,512]{1,0:T(8,128)}), f32[1280,512]{1,0:T(8,128)}) %all-gather.3.cloned.1.call-update) | async-done | bytes 2621456 | tf_op jit(solution)/shard_map/all_gather | solution.py:309
  88.6 10.1 %apply_inverse.1 = (f32[28,512]{1,0:T(8,128)}, f32[448,896]{1,0:T(8,128)}, f32[16,320]{1,0:T(8,128)}, f32[320,448]{1,0:T(8,128)}) custom-call(s32[1]{0:T(128)} %bitcast.col_ref, bf16[512,512]{1,0:T(8,128)(2,1)S(1)} %get-tuple-element.16.high_hbm, bf16[512,512]{1,0:T(8,128)(2,1)S(1)} %get-tuple-element.17.low_hbm, ...), custom_call_target="tpu_custom_call" | custom-call | flops 4000000000 | bytes 10000000 | tf_op jit(solution)/shard_map/apply_inverse/pallas_call | solution.py:272
  (1 shorter events, 0.0 us)
Async XLA Ops:
  7.2 81.4 %all-gather.3.cloned.1.call-start = ((), (), s32[]{:S(2)}) async-start(), calls=%async_computation.3 | async-start | bytes 2703360 | tf_op jit(solution)/shard_map/all_gather | solution.py:309
  7.2 0.8 copy-start
  8.1 0.7 copy-start.1
  42.8 21.9 %all-to-all-start.1 = ((f32[16,32,512]{2,1,0:T(8,128)}), f32[16,32,512]{2,1,0:T(8,128)S(1)}, u32[]{:S(2)}, u32[]{:S(2)}) async-start(f32[16,32,512]{2,1,0:T(8,128)} %copy_out.1), calls=%async_computation.1 | async-start | bytes 2097152 | tf_op jit(solution)/shard_map/all_to_all | solution.py:313
  64.7 18.8 %all-to-all-start.2 = ((f32[16,28,512]{2,1,0:T(8,128)}), f32[16,28,512]{2,1,0:T(8,128)S(1)}, u32[]{:S(2)}, u32[]{:S(2)}) async-start(f32[16,28,512]{2,1,0:T(8,128)} %get-tuple-element.18), calls=%async_computation.2 | async-start | bytes 2097152 | tf_op jit(solution)/shard_map/all_to_all | solution.py:315
Sparse Core Ops, SparseCore 0:
  10.7 77.8 all-gather.2

commit v5 on v4

--- a/solution.py
+++ b/solution.py
@@ -137,32 +137,42 @@
     )(block)
 
 
-def pack_kernel(panel_ref, truth_ref, packed_ref, copies_hbm, sem):
-    copies = [pltpu.make_async_copy(panel_ref, copies_hbm.at[i], sem.at[i]) for i in range(16)]
-    for copy in copies:
-        copy.start()
-    packed_ref[0:8, 0:256] = truth_ref[0:8, 0:256]
-    packed_ref[0:8, 256:512] = truth_ref[8:16, 0:256]
-    packed_ref[8:12, :] = jnp.zeros((4, 512), jnp.float32)
+def pack_kernel(panel_hbm, truth_hbm, packed_hbm, panel, truth, packed, sem):
+    first = pltpu.make_async_copy(panel_hbm, panel, sem.at[0])
+    second = pltpu.make_async_copy(truth_hbm, truth, sem.at[1])
+    first.start()
+    second.start()
+    second.wait()
+    packed[28:32, :] = jnp.zeros((4, 512), jnp.float32)
     for q in range(4):
-        packed_ref[8:12, 128 * q:128 * q + 64] = truth_ref[4 * q:4 * q + 4, 256:320]
-    packed_ref[12:40, :] = panel_ref[...]
-    for copy in copies:
-        copy.wait()
+        packed[28:32, 128 * q:128 * q + 64] = truth[4 * q:4 * q + 4, 256:320]
+    packed[32:40, 0:256] = truth[0:8, 0:256]
+    packed[32:40, 256:512] = truth[8:16, 0:256]
+    first.wait()
+    packed[0:28, :] = panel[...]
+    store = pltpu.make_async_copy(packed, packed_hbm, sem.at[2])
+    store.start()
+    store.wait()
 
 
 def pack(panel, truth):
     f32 = jnp.float32
-    whole = pl.BlockSpec(memory_space=pltpu.VMEM)
+    hbm = pl.BlockSpec(memory_space=pltpu.HBM)
+    keep = pltpu.with_memory_space_constraint
     return pl.pallas_call(
         pack_kernel,
-        out_shape=(jax.ShapeDtypeStruct((40, 512), f32), jax.ShapeDtypeStruct((16, 28, 512), f32)),
-        in_specs=[whole, whole],
-        out_specs=(whole, pl.BlockSpec(memory_space=pl.ANY)),
-        scratch_shapes=[pltpu.SemaphoreType.DMA((16,))],
-        compiler_params=pltpu.CompilerParams(vmem_limit_bytes=4 * 2**20),
+        out_shape=jax.ShapeDtypeStruct((40, 512), f32),
+        in_specs=[hbm, hbm],
+        out_specs=hbm,
+        scratch_shapes=[
+            pltpu.VMEM((28, 512), f32),
+            pltpu.VMEM((16, 320), f32),
+            pltpu.VMEM((40, 512), f32),
+            pltpu.SemaphoreType.DMA((3,)),
+        ],
+        compiler_params=pltpu.CompilerParams(vmem_limit_bytes=2 * 2**20),
         name="pack",
-    )(panel, truth)
+    )(keep(panel, pltpu.HBM), keep(truth, pltpu.HBM))
 
 
 def copy_kernel(strip_ref, copies_hbm, sem):
@@ -185,138 +195,178 @@
     )(strip)
 
 
-def thrice(a_high, a_low, b_high, b_low, dims):
+def thrice(a, b, dims):
     dot = lambda p, q: lax.dot_general(p, q, dims, preferred_element_type=jnp.float32)
-    return dot(a_high, b_high) + dot(a_high, b_low) + dot(a_low, b_high)
+    return dot(a[0], b[0]) + dot(a[0], b[1]) + dot(a[1], b[0])
+
+
+def solve(rows, high, low):
+    top = (high[:256, :256], low[:256, :256])
+    low_left = (high[256:, :], low[256:, :])
+    a = thrice((rows[0][:, :256], rows[1][:, :256]), top, NT)
+    return jnp.concatenate([a, thrice(rows, low_left, NT)], 1)
+
+
+def dealt_kernel(high_any, low_any, dealt_any, panel_hbm, d_high_any, d_low_any, factor_hbm, high, low, dealt, stack, d_high, d_low, factor, sem):
+    loads = [
+        pltpu.make_async_copy(src, dst, sem.at[i])
+        for i, (src, dst) in enumerate(
+            [(high_any, high), (low_any, low), (dealt_any, dealt), (panel_hbm, factor)]
+        )
+    ]
+    for load in loads:
+        load.start()
+    for load in loads:
+        load.wait()
+    for r in range(16):
+        stack[28 * r:28 * r + 28, :] = dealt[r]
+    stack[448:476, :] = factor[...]
+    stack[476:480, :] = jnp.zeros((4, 512), jnp.float32)
+    done = solve(halves(stack[...]), high, low)
+    factor[...] = done[448:476, :]
+    d_high[...], d_low[...] = halves(done[:448, :])
+    stores = [
+        pltpu.make_async_copy(src, dst, sem.at[4 + i])
+        for i, (src, dst) in enumerate([(factor, factor_hbm), (d_high, d_high_any), (d_low, d_low_any)])
+    ]
+    for store in stores:
+        store.start()
+    for store in stores:
+        store.wait()
+
+
+def solve_dealt(high, low, dealt, panel):
+    f32, bf16 = jnp.float32, jnp.bfloat16
+    anywhere, hbm = pl.BlockSpec(memory_space=pl.ANY), pl.BlockSpec(memory_space=pltpu.HBM)
+    half = jax.ShapeDtypeStruct((448, 512), bf16)
+    return pl.pallas_call(
+        dealt_kernel,
+        out_shape=(half, half, jax.ShapeDtypeStruct((28, 512), f32)),
+        in_specs=[anywhere] * 3 + [hbm],
+        out_specs=(anywhere, anywhere, hbm),
+        scratch_shapes=[
+            pltpu.VMEM((512, 512), bf16),
+            pltpu.VMEM((512, 512), bf16),
+            pltpu.VMEM((16, 28, 512), f32),
+            pltpu.VMEM((480, 512), f32),
+            pltpu.VMEM((448, 512), bf16),
+            pltpu.VMEM((448, 512), bf16),
+            pltpu.VMEM((28, 512), f32),
+            pltpu.SemaphoreType.DMA((7,)),
+        ],
+        compiler_params=pltpu.CompilerParams(vmem_limit_bytes=12 * 2**20),
+        cost_estimate=pl.CostEstimate(flops=10**9, bytes_accessed=2 * 10**6, transcendentals=0),
+        name="solve_dealt",
+    )(high, low, dealt, pltpu.with_memory_space_constraint(panel, pltpu.HBM))
 
 
 def apply_kernel(
-    col_ref, high_hbm, low_hbm, dealt_hbm, gathered_hbm, panel_hbm, trailing_hbm, rest_hbm,
-    factor_hbm, updated_hbm, solved_hbm, truth_hbm,
-    inv_high, inv_low, dealt, gathered, panel, trailing, rest,
-    row_high, row_low, truth, x_high, x_low, factor, solved, sem, out_sem,
+    col_ref, high_any, low_any, d_high_any, d_low_any, gathered_hbm, trailing_hbm, rest_hbm,
+    updated_hbm, solved_hbm, truth_hbm,
+    high, low, d_high, d_low, gathered, trailing, rest, stack, truth, solved, sem, out_sem,
 ):
     loads = [
         pltpu.make_async_copy(src, dst, sem.at[i])
         for i, (src, dst) in enumerate(
             [
-                (high_hbm, inv_high), (low_hbm, inv_low), (dealt_hbm, dealt), (gathered_hbm, gathered),
-                (panel_hbm, panel), (trailing_hbm, trailing), (rest_hbm, rest),
+                (gathered_hbm.at[0:19], gathered.at[0:19]), (high_any, high), (low_any, low),
+                (d_high_any, d_high), (d_low_any, d_low),
+                (trailing_hbm, trailing), (gathered_hbm.at[19:32], gathered.at[19:32]), (rest_hbm, rest),
             ]
         )
     ]
     for load in loads:
         load.start()
-    loads[0].wait()
-    loads[1].wait()
-
-    def solve(high, low):
-        a = thrice(high[:, :256], low[:, :256], inv_high[:256, :256], inv_low[:256, :256], NT)
-        b = thrice(high, low, inv_high[256:, :], inv_low[256:, :], NT)
-        return jnp.concatenate([a, b], 1)
-
-    loads[2].wait()
-    for r in range(16):
-        row_high[28 * r:28 * r + 28, :] = dealt[r]
-    high, low = halves(row_high[...])
-    done = solve(high, low)
-    d_high, d_low = halves(done)
-    loads[3].wait()
-    loads[4].wait()
-    stack = row_low
-    for c in range(32):
-        stack[28 * c:28 * c + 28, :] = gathered[c, 12:40, :]
-        truth[16 * c:16 * c + 8, 0:256] = gathered[c, 0:8, 0:256]
-        truth[16 * c + 8:16 * c + 16, 0:256] = gathered[c, 0:8, 256:512]
-        for q in range(4):
-            truth[16 * c + 4 * q:16 * c + 4 * q + 4, 256:384] = gathered[c, 8:12, 128 * q:128 * q + 128]
-    stack[896:1216, :] = truth[...].T[0:320, :]
-    stack[1216:1244, :] = panel[...]
-    stack[1244:1248, :] = jnp.zeros((4, 512), jnp.float32)
-    at = pl.ds(pl.multiple_of(col_ref[0] * 16, 16), 16)
-    i_high, i_low = inv_high[at, :], inv_low[at, :]
-    t_high, t_low = halves(stack[896:1216, :])
-    solved[...] = thrice(i_high, i_low, t_high, t_low, NT)
-    for lo, hi in ((0, 416), (416, 832), (832, 1248)):
-        high, low = halves(stack[lo:hi, :])
-        part = solve(high, low)
-        if hi == 1248:
-            factor[...] = part[1216 - lo:1244 - lo, :]
-        x_high[lo:hi, :], x_low[lo:hi, :] = halves(part)
-    stores = [
-        pltpu.make_async_copy(factor, factor_hbm, out_sem.at[0]),
-        pltpu.make_async_copy(solved, solved_hbm, out_sem.at[1]),
-    ]
-    for store in stores:
-        store.start()
-    loads[5].wait()
-    for i in range(4):
-        a = slice(112 * i, 112 * i + 112)
-        trailing[a, :] = trailing[a, :] - thrice(d_high[a], d_low[a], x_high[:896, :], x_low[:896, :], NT)
-        store = pltpu.make_async_copy(trailing.at[a], updated_hbm.at[a], out_sem.at[2 + i])
+    for load in loads[:3]:
+        load.wait()
+    stores = []
+
+    def unpack(first, last):
+        for c in range(first, last):
+            stack[28 * c:28 * c + 28, :] = gathered[c, 0:28, :]
+            truth[16 * c:16 * c + 8, 0:256] = gathered[c, 32:40, 0:256]
+            truth[16 * c + 8:16 * c + 16, 0:256] = gathered[c, 32:40, 256:512]
+            for q in range(4):
+                truth[16 * c + 4 * q:16 * c + 4 * q + 4, 256:384] = gathered[c, 28:32, 128 * q:128 * q + 128]
+
+    def put(src, dst):
+        store = pltpu.make_async_copy(src, dst, out_sem.at[len(stores)])
         store.start()
         stores.append(store)
+
+    def update(first, last):
+        rows = halves(solve(halves(stack[first:last, :]), high, low))
+        dealt = (d_high[...], d_low[...])
+        trailing[:, first:last] = trailing[:, first:last] - thrice(dealt, rows, NT)
+        put(trailing.at[:, first:last], updated_hbm.at[:, first:last])
+
+    unpack(0, 19)
+    for load in loads[3:6]:
+        load.wait()
+    update(0, 512)
     loads[6].wait()
-    rest[...] = rest[...] - thrice(x_high[896:1216, :], x_low[896:1216, :], d_high, d_low, NT)
-    store = pltpu.make_async_copy(rest, truth_hbm, out_sem.at[6])
-    store.start()
-    stores.append(store)
+    unpack(19, 32)
+    update(512, 896)
+    columns = halves(truth[...].T[0:320, :])
+    at = pl.ds(pl.multiple_of(col_ref[0] * 16, 16), 16)
+    solved[...] = thrice((high[at, :], low[at, :]), columns, NT)
+    put(solved, solved_hbm)
+    rows = halves(solve(columns, high, low))
+    loads[7].wait()
+    rest[...] = rest[...] - thrice(rows, (d_high[...], d_low[...]), NT)
+    put(rest, truth_hbm)
     for store in stores:
         store.wait()
 
 
-def apply_inverse(column, high, low, dealt, gathered, panel, trailing, rest):
+def apply_inverse(column, high, low, d_high, d_low, gathered, trailing, rest):
     f32, bf16 = jnp.float32, jnp.bfloat16
-    anywhere = pl.BlockSpec(memory_space=pl.ANY)
+    anywhere, hbm = pl.BlockSpec(memory_space=pl.ANY), pl.BlockSpec(memory_space=pltpu.HBM)
     keep = pltpu.with_memory_space_constraint
     return pl.pallas_call(
         apply_kernel,
         out_shape=(
-            jax.ShapeDtypeStruct((28, 512), f32),
             jax.ShapeDtypeStruct((448, 896), f32),
             jax.ShapeDtypeStruct((16, 320), f32),
             jax.ShapeDtypeStruct((320, 448), f32),
         ),
-        in_specs=[pl.BlockSpec(memory_space=pltpu.SMEM)] + [anywhere] * 3 + [pl.BlockSpec(memory_space=pltpu.HBM)] * 4,
-        out_specs=(pl.BlockSpec(memory_space=pltpu.HBM),) * 4,
+        in_specs=[pl.BlockSpec(memory_space=pltpu.SMEM)] + [anywhere] * 4 + [hbm] * 3,
+        out_specs=(hbm,) * 3,
         scratch_shapes=[
             pltpu.VMEM((512, 512), bf16),
             pltpu.VMEM((512, 512), bf16),
-            pltpu.VMEM((16, 28, 512), f32),
+            pltpu.VMEM((448, 512), bf16),
+            pltpu.VMEM((448, 512), bf16),
             pltpu.VMEM((32, 40, 512), f32),
-            pltpu.VMEM((28, 512), f32),
             pltpu.VMEM((448, 896), f32),
             pltpu.VMEM((320, 448), f32),
-            pltpu.VMEM((448, 512), f32),
-            pltpu.VMEM((1248, 512), f32),
+            pltpu.VMEM((896, 512), f32),
             pltpu.VMEM((512, 384), f32),
-            pltpu.VMEM((1248, 512), bf16),
-            pltpu.VMEM((1248, 512), bf16),
-            pltpu.VMEM((28, 512), f32),
             pltpu.VMEM((16, 320), f32),
-            pltpu.SemaphoreType.DMA((7,)),
-            pltpu.SemaphoreType.DMA((7,)),
+            pltpu.SemaphoreType.DMA((8,)),
+            pltpu.SemaphoreType.DMA((4,)),
         ],
         compiler_params=pltpu.CompilerParams(vmem_limit_bytes=24 * 2**20),
         cost_estimate=pl.CostEstimate(flops=4 * 10**9, bytes_accessed=10**7, transcendentals=0),
         name="apply_inverse",
-    )(column, high, low, dealt, *(keep(x, pltpu.HBM) for x in (gathered, panel, trailing, rest)))
+    )(column, high, low, d_high, d_low, *(keep(x, pltpu.HBM) for x in (gathered, trailing, rest)))
 
 
 def per_device(diag_block, panel, trailing, truth_panel, truth_rest):
     rows, columns = ("x", "y"), ("z", "k")
-    packed, copies = pack(panel, truth_panel.T)
+    packed = pack(panel, truth_panel.T)
     gathered = lax.all_gather(packed, columns, axis=0, tiled=False)
     small = jnp.broadcast_to(diag_block.reshape(1, 4, 128), (32, 4, 128))
     pieces = lax.all_to_all(small, columns, 0, 0)
     strip = pieces.reshape(32, 4, 8, 16).transpose(1, 2, 0, 3).reshape(32, 512)
     whole = lax.all_to_all(copy_out(strip), rows, 0, 0).reshape(512, 512)
-    copies, whole = lax.optimization_barrier((copies, whole))
+    copies, whole = lax.optimization_barrier((copy_out(panel), whole))
     dealt = lax.all_to_all(copies, rows, 0, 0)
     high, low = invert_factor(whole)
     column = (lax.axis_index("z") * 2 + lax.axis_index("k")).astype(jnp.int32)[None]
-    factor, updated, solved, truth_updated = apply_inverse(
-        column, high, low, dealt, gathered, panel, trailing.T, truth_rest
+    d_high, d_low, factor = solve_dealt(high, low, dealt, panel)
+    updated, solved, truth_updated = apply_inverse(
+        column, high, low, d_high, d_low, gathered, trailing.T, truth_rest
     )
     return factor, updated.T, solved.T, truth_updated
 

time: 106 us -> 105 us (level)
  Pallas kernels: 26.5 us -> 28.9 us
  waiting for transfers between devices: 21.3 us -> 19.2 us
  local copies, waits for them, and re-layouts: 3.06 us -> 1.5 us
    unnamed x5 -> x3, local copies, waits for them, and re-layouts: 2.34 us -> 0.78 us
    pallas_call x2 -> x3, Pallas kernels: 11.8 us -> 13.1 us  [the longest x1 9.11 us: apply_inverse(): pl.pallas_call(apply_kernel, out_shape=(jax.ShapeDtypeStruct((448, 896),...]
    all_to_all x1, waiting for transfers between devices: 15.1 us -> 13.9 us  [per_device(): whole = lax.all_to_all(copy_out(strip), rows, 0, 0).reshape(512, 512)]
    pallas_call x1 -> x2, Pallas kernels: 1.09 us -> 2.24 us  [copy_out(): pl.pallas_call(copy_kernel, out_shape=jax.ShapeDtypeStruct((16,) + strip....]
  transfers between devices with their start and end apart: 3 -> 3, of which waited for: 3 -> 3; matrix products, arithmetic and copies ran while one was open for 1% -> 1% of each run, Pallas kernels for 14% -> 18%
where the time goes in v5:
time: 105 us; the launch traced here: 104 us
  blocking collectives  29.6 us (28%)
  Pallas kernels  28.9 us (28%)
  waiting for transfers between devices  19.2 us (18%)
  between operations  14.1 us (13%)
  starting transfers between devices  11.1 us (11%)
  local copies, waits for them, and re-layouts  1.5 us (1%)
    all_to_all x1, blocking collectives, per_device(): pieces = lax.all_to_all(small, columns, 0, 0)  29.6 us
    all_to_all x1, waiting for transfers between devices, per_device(): whole = lax.all_to_all(copy_out(strip), rows, 0, 0).reshape(512, 512)  13.9 us
    pallas_call x1, Pallas kernels, invert_factor(): pl.pallas_call(invert_kernel, out_shape=(half, half), in_specs=[anywhere]...  13.6 us
    pallas_call x1, Pallas kernels, apply_inverse(): pl.pallas_call(apply_kernel, out_shape=(jax.ShapeDtypeStruct((448, 896),...  9.11 us
    all_to_all x1, starting transfers between devices, per_device(): whole = lax.all_to_all(copy_out(strip), rows, 0, 0).reshape(512, 512)  6.76 us
    all_gather x1, waiting for transfers between devices, per_device(): gathered = lax.all_gather(packed, columns, axis=0, tiled=False)  4.31 us
    all_to_all x1, starting transfers between devices, per_device(): dealt = lax.all_to_all(copies, rows, 0, 0)  4.31 us
    pallas_call x1, Pallas kernels, solve_dealt(): pl.pallas_call(dealt_kernel, out_shape=(half, half, jax.ShapeDtypeStruct(...  2.47 us
  transfers between devices with their start and end apart: 3, of which 3 were waited for; matrix products, arithmetic and copies ran while one was open for 1% of the time, Pallas kernels for 18%

profile of v5, /device:TPU:1, one launch (start us, length us, event | category | flops | bytes accessed | tf_op | source)
XLA Modules:
  0.0 104.4 jit_solution(803305794045021180)
XLA Ops:
  7.2 0.0 all-gather.3.cloned.1.call-start
  7.2 1.5 %pack.1 = f32[40,512]{1,0:T(8,128)} custom-call(f32[28,512]{1,0:T(8,128)} %panel_hbm.3, f32[16,320]{1,0:T(8,128)} %bitcast.14), custom_call_target="tpu_custom_call" | custom-call | tf_op jit(solution)/shard_map/pack/pallas_call | solution.py:162
  8.7 0.0 all-gather.3.cloned.1.call-update
  8.7 0.8 copy.11
  9.5 0.1 broadcast_in_dim.10
  9.6 29.6 %all_to_all.15 = f32[32,4,128]{2,1,0:T(4,128)S(1)} all-to-all(f32[32,4,128]{2,1,0:T(4,128)S(1)} %broadcast_in_dim.11), channel_id=1, replica_groups=mesh['x'=4,'y'=4,'z'=16,'k'=2] {'z','k'}, dimensions={0} | all-to-all | bytes 131072 | tf_op jit(solution)/shard_map/all_to_all | solution.py:360
  39.2 0.1 copy.12
  39.3 0.2 copy.13
  39.5 0.3 reshape.20.strip_ref
  39.8 0.0 copy-start
  39.8 1.1 %copy_out.3 = f32[16,32,512]{2,1,0:T(8,128)} custom-call(f32[32,512]{1,0:T(8,128)S(1)} %reshape.20.strip_ref), custom_call_target="tpu_custom_call" | custom-call | tf_op jit(solution)/shard_map/copy_out/pallas_call | solution.py:187
  40.9 6.8 %all-to-all-start.1 = ((f32[16,32,512]{2,1,0:T(8,128)}), f32[16,32,512]{2,1,0:T(8,128)S(1)}, u32[]{:S(2)}, u32[]{:S(2)}) async-start(f32[16,32,512]{2,1,0:T(8,128)} %copy_out.3), calls=%async_computation.1 | async-start | bytes 2097152 | tf_op jit(solution)/shard_map/all_to_all | solution.py:362
  47.7 0.0 copy-done
  47.7 1.1 %copy_out.2 = f32[16,28,512]{2,1,0:T(8,128)} custom-call(f32[28,512]{1,0:T(8,128)S(1)} %copy-done), custom_call_target="tpu_custom_call" | custom-call | tf_op jit(solution)/shard_map/copy_out/pallas_call | solution.py:187
  48.9 13.9 %all-to-all-done.1 = f32[16,32,512]{2,1,0:T(8,128)S(1)} async-done(((f32[16,32,512]{2,1,0:T(8,128)}), f32[16,32,512]{2,1,0:T(8,128)S(1)}, u32[]{:S(2)}, u32[]{:S(2)}) %all-to-all-start.1) | async-done | bytes 1048608 | tf_op jit(solution)/shard_map/all_to_all | solution.py:362
  62.7 4.3 %all-to-all-start.2 = ((f32[16,28,512]{2,1,0:T(8,128)}), f32[16,28,512]{2,1,0:T(8,128)S(1)}, u32[]{:S(2)}, u32[]{:S(2)}) async-start(f32[16,28,512]{2,1,0:T(8,128)} %copy_out.2), calls=%async_computation.2 | async-start | bytes 2097152 | tf_op jit(solution)/shard_map/all_to_all | solution.py:364
  67.0 13.6 %invert_factor.1 = (bf16[512,512]{1,0:T(8,128)(2,1)S(1)}, bf16[512,512]{1,0:T(8,128)(2,1)S(1)}) custom-call(f32[512,512]{1,0:T(8,128)S(1)} %bitcast.12), custom_call_target="tpu_custom_call" | custom-call | flops 10000000000 | bytes 2000000 | tf_op jit(solution)/shard_map/invert_factor/pallas_call | solution.py:120
  80.6 1.0 all-to-all-done.2.dealt_any
  81.6 2.5 %solve_dealt.1 = (bf16[448,512]{1,0:T(8,128)(2,1)S(1)}, bf16[448,512]{1,0:T(8,128)(2,1)S(1)}, f32[28,512]{1,0:T(8,128)}) custom-call(bf16[512,512]{1,0:T(8,128)(2,1)S(1)} %get-tuple-element.15.high_any, bf16[512,512]{1,0:T(8,128)(2,1)S(1)} %get-tuple-element.16.low_any, f32[16,28,512]{2,1,0:T(8,128)S(1)} %all-to-all-done.2.dealt_any, f32[28,512]{1,0:T(8,128)} %panel_hbm.3), custom_call_target="tpu_custom_call" | custom-call | flops 1000000000 | bytes 2000000 | tf_op jit(solution)/shard_map/solve_dealt/pallas_call | solution.py:242
  84.1 4.3 %all-gather.3.cloned.1.call-done = f32[1280,512]{1,0:T(8,128)} async-done(((f32[40,512]{1,0:T(8,128)}), f32[1280,512]{1,0:T(8,128)}) %all-gather.3.cloned.1.call-update) | async-done | bytes 2621456 | tf_op jit(solution)/shard_map/all_gather | solution.py:358
  88.4 9.1 %apply_inverse.1 = (f32[448,896]{1,0:T(8,128)}, f32[16,320]{1,0:T(8,128)}, f32[320,448]{1,0:T(8,128)}) custom-call(s32[1]{0:T(128)} %bitcast.3.col_ref, bf16[512,512]{1,0:T(8,128)(2,1)S(1)} %get-tuple-element.15.high_any, bf16[512,512]{1,0:T(8,128)(2,1)S(1)} %get-tuple-element.16.low_any, bf16[448,512]{1,0:T(8,128)(2,1)S(1)} %get-tuple-element.19.d_high_any, ...), custom_call_target="tpu_custom_call" | custom-call | flops 4000000000 | bytes 10000000 | tf_op jit(solution)/shard_map/apply_inverse/pallas_call | solution.py:326
  (1 shorter events, 0.0 us)
Async XLA Ops:
  7.2 81.3 %all-gather.3.cloned.1.call-start = ((), (), s32[]{:S(2)}) async-start(), calls=%async_computation.3 | async-start | bytes 2703360 | tf_op jit(solution)/shard_map/all_gather | solution.py:358
  39.8 7.9 %copy-start = (f32[28,512]{1,0:T(8,128)S(1)}, f32[28,512]{1,0:T(8,128)}, u32[]{:S(2)}) copy-start(f32[28,512]{1,0:T(8,128)} %panel_hbm.3) | copy-start | bytes 172036
  40.9 21.8 %all-to-all-start.1 = ((f32[16,32,512]{2,1,0:T(8,128)}), f32[16,32,512]{2,1,0:T(8,128)S(1)}, u32[]{:S(2)}, u32[]{:S(2)}) async-start(f32[16,32,512]{2,1,0:T(8,128)} %copy_out.3), calls=%async_computation.1 | async-start | bytes 2097152 | tf_op jit(solution)/shard_map/all_to_all | solution.py:362
  62.7 18.9 %all-to-all-start.2 = ((f32[16,28,512]{2,1,0:T(8,128)}), f32[16,28,512]{2,1,0:T(8,128)S(1)}, u32[]{:S(2)}, u32[]{:S(2)}) async-start(f32[16,28,512]{2,1,0:T(8,128)} %copy_out.2), calls=%async_computation.2 | async-start | bytes 2097152 | tf_op jit(solution)/shard_map/all_to_all | solution.py:364
Sparse Core Ops, SparseCore 0:
  10.7 77.7 all-gather.2

commit v6 on v5

--- a/solution.py
+++ b/solution.py
@@ -72,7 +72,7 @@
                 m[i] = acc
 
 
-def invert_kernel(a_hbm, high_hbm, low_hbm, m_ref, d_ref, t_ref, o_ref, high_ref, low_ref, sem):
+def invert_kernel(a_hbm, inverse_hbm, m_ref, d_ref, t_ref, o_ref, sem):
     nb, n = 128, 512
     load = pltpu.make_async_copy(a_hbm, m_ref, sem.at[0])
     load.start()
@@ -102,34 +102,25 @@
         return carry
 
     lax.fori_loop(0, n // nb, step, 0)
-    high_ref[...], low_ref[...] = halves(o_ref[...])
-    stores = [
-        pltpu.make_async_copy(high_ref, high_hbm, sem.at[1]),
-        pltpu.make_async_copy(low_ref, low_hbm, sem.at[2]),
-    ]
-    for store in stores:
-        store.start()
-    for store in stores:
-        store.wait()
+    store = pltpu.make_async_copy(o_ref, inverse_hbm, sem.at[1])
+    store.start()
+    store.wait()
 
 
 def invert_factor(block):
     n = block.shape[0]
     anywhere = pl.BlockSpec(memory_space=pl.ANY)
-    half = jax.ShapeDtypeStruct((n, n), jnp.bfloat16)
     return pl.pallas_call(
         invert_kernel,
-        out_shape=(half, half),
+        out_shape=jax.ShapeDtypeStruct((n, n), jnp.float32),
         in_specs=[anywhere],
-        out_specs=(anywhere, anywhere),
+        out_specs=anywhere,
         scratch_shapes=[
             pltpu.VMEM((n, n), jnp.float32),
             pltpu.VMEM((128, 128), jnp.float32),
             pltpu.VMEM((128, 128), jnp.float32),
             pltpu.VMEM((n, n), jnp.float32),
-            pltpu.VMEM((n, n), jnp.bfloat16),
-            pltpu.VMEM((n, n), jnp.bfloat16),
-            pltpu.SemaphoreType.DMA((3,)),
+            pltpu.SemaphoreType.DMA((2,)),
         ],
         compiler_params=pltpu.CompilerParams(vmem_limit_bytes=16 * 2**20),
         cost_estimate=pl.CostEstimate(flops=10**10, bytes_accessed=2 * 10**6, transcendentals=0),
@@ -200,34 +191,32 @@
     return dot(a[0], b[0]) + dot(a[0], b[1]) + dot(a[1], b[0])
 
 
-def solve(rows, high, low):
-    top = (high[:256, :256], low[:256, :256])
-    low_left = (high[256:, :], low[256:, :])
-    a = thrice((rows[0][:, :256], rows[1][:, :256]), top, NT)
-    return jnp.concatenate([a, thrice(rows, low_left, NT)], 1)
-
-
-def dealt_kernel(high_any, low_any, dealt_any, panel_hbm, d_high_any, d_low_any, factor_hbm, high, low, dealt, stack, d_high, d_low, factor, sem):
+def dealt_kernel(inverse_any, dealt_any, panel_hbm, w_high_any, w_low_any, factor_hbm, inverse, dealt, stack, w_high, w_low, factor, sem):
     loads = [
         pltpu.make_async_copy(src, dst, sem.at[i])
-        for i, (src, dst) in enumerate(
-            [(high_any, high), (low_any, low), (dealt_any, dealt), (panel_hbm, factor)]
-        )
+        for i, (src, dst) in enumerate([(dealt_any, dealt), (panel_hbm, factor), (inverse_any, inverse)])
     ]
     for load in loads:
         load.start()
-    for load in loads:
-        load.wait()
+    loads[0].wait()
+    loads[1].wait()
     for r in range(16):
         stack[28 * r:28 * r + 28, :] = dealt[r]
     stack[448:476, :] = factor[...]
     stack[476:480, :] = jnp.zeros((4, 512), jnp.float32)
-    done = solve(halves(stack[...]), high, low)
-    factor[...] = done[448:476, :]
-    d_high[...], d_low[...] = halves(done[:448, :])
+    loads[2].wait()
+    dot = lambda p, q, dims: lax.dot_general(p, q, dims, precision=HI, preferred_element_type=jnp.float32)
+    left = dot(stack[:, :256], inverse[:256, :256], NT)
+    right = dot(stack[...], inverse[256:, :], NT)
+    factor[:, :256] = left[448:476, :]
+    factor[:, 256:] = right[448:476, :]
+    w_left = dot(left[:448], inverse[:256, :256], NN) + dot(right[:448], inverse[256:, :256], NN)
+    w_right = dot(right[:448], inverse[256:, 256:], NN)
+    w_high[:, :256], w_low[:, :256] = halves(w_left)
+    w_high[:, 256:], w_low[:, 256:] = halves(w_right)
     stores = [
-        pltpu.make_async_copy(src, dst, sem.at[4 + i])
-        for i, (src, dst) in enumerate([(factor, factor_hbm), (d_high, d_high_any), (d_low, d_low_any)])
+        pltpu.make_async_copy(src, dst, sem.at[3 + i])
+        for i, (src, dst) in enumerate([(factor, factor_hbm), (w_high, w_high_any), (w_low, w_low_any)])
     ]
     for store in stores:
         store.start()
@@ -235,50 +224,48 @@
         store.wait()
 
 
-def solve_dealt(high, low, dealt, panel):
+def solve_dealt(inverse, dealt, panel):
     f32, bf16 = jnp.float32, jnp.bfloat16
     anywhere, hbm = pl.BlockSpec(memory_space=pl.ANY), pl.BlockSpec(memory_space=pltpu.HBM)
     half = jax.ShapeDtypeStruct((448, 512), bf16)
     return pl.pallas_call(
         dealt_kernel,
         out_shape=(half, half, jax.ShapeDtypeStruct((28, 512), f32)),
-        in_specs=[anywhere] * 3 + [hbm],
+        in_specs=[anywhere] * 2 + [hbm],
         out_specs=(anywhere, anywhere, hbm),
         scratch_shapes=[
-            pltpu.VMEM((512, 512), bf16),
-            pltpu.VMEM((512, 512), bf16),
+            pltpu.VMEM((512, 512), f32),
             pltpu.VMEM((16, 28, 512), f32),
             pltpu.VMEM((480, 512), f32),
             pltpu.VMEM((448, 512), bf16),
             pltpu.VMEM((448, 512), bf16),
             pltpu.VMEM((28, 512), f32),
-            pltpu.SemaphoreType.DMA((7,)),
+            pltpu.SemaphoreType.DMA((6,)),
         ],
-        compiler_params=pltpu.CompilerParams(vmem_limit_bytes=12 * 2**20),
+        compiler_params=pltpu.CompilerParams(vmem_limit_bytes=16 * 2**20),
         cost_estimate=pl.CostEstimate(flops=10**9, bytes_accessed=2 * 10**6, transcendentals=0),
         name="solve_dealt",
-    )(high, low, dealt, pltpu.with_memory_space_constraint(panel, pltpu.HBM))
+    )(inverse, dealt, pltpu.with_memory_space_constraint(panel, pltpu.HBM))
 
 
 def apply_kernel(
-    col_ref, high_any, low_any, d_high_any, d_low_any, gathered_hbm, trailing_hbm, rest_hbm,
+    col_ref, inverse_any, w_high_any, w_low_any, gathered_hbm, trailing_hbm, rest_hbm,
     updated_hbm, solved_hbm, truth_hbm,
-    high, low, d_high, d_low, gathered, trailing, rest, stack, truth, solved, sem, out_sem,
+    own, w_high, w_low, gathered, trailing, rest, stack, truth, solved, sem, out_sem,
 ):
+    at = pl.ds(pl.multiple_of(col_ref[0] * 16, 16), 16)
     loads = [
         pltpu.make_async_copy(src, dst, sem.at[i])
         for i, (src, dst) in enumerate(
             [
-                (gathered_hbm.at[0:19], gathered.at[0:19]), (high_any, high), (low_any, low),
-                (d_high_any, d_high), (d_low_any, d_low),
-                (trailing_hbm, trailing), (gathered_hbm.at[19:32], gathered.at[19:32]), (rest_hbm, rest),
+                (gathered_hbm.at[0:19], gathered.at[0:19]), (w_high_any, w_high), (w_low_any, w_low),
+                (trailing_hbm, trailing), (gathered_hbm.at[19:32], gathered.at[19:32]),
+                (inverse_any.at[at], own), (rest_hbm, rest),
             ]
         )
     ]
     for load in loads:
         load.start()
-    for load in loads[:3]:
-        load.wait()
     stores = []
 
     def unpack(first, last):
@@ -295,31 +282,30 @@
         stores.append(store)
 
     def update(first, last):
-        rows = halves(solve(halves(stack[first:last, :]), high, low))
-        dealt = (d_high[...], d_low[...])
-        trailing[:, first:last] = trailing[:, first:last] - thrice(dealt, rows, NT)
+        rows = halves(stack[first:last, :])
+        trailing[:, first:last] = trailing[:, first:last] - thrice((w_high[...], w_low[...]), rows, NT)
         put(trailing.at[:, first:last], updated_hbm.at[:, first:last])
 
+    loads[0].wait()
     unpack(0, 19)
-    for load in loads[3:6]:
+    for load in loads[1:4]:
         load.wait()
     update(0, 512)
-    loads[6].wait()
+    loads[4].wait()
     unpack(19, 32)
     update(512, 896)
     columns = halves(truth[...].T[0:320, :])
-    at = pl.ds(pl.multiple_of(col_ref[0] * 16, 16), 16)
-    solved[...] = thrice((high[at, :], low[at, :]), columns, NT)
+    loads[5].wait()
+    solved[...] = thrice(halves(own[...]), columns, NT)
     put(solved, solved_hbm)
-    rows = halves(solve(columns, high, low))
-    loads[7].wait()
-    rest[...] = rest[...] - thrice(rows, (d_high[...], d_low[...]), NT)
+    loads[6].wait()
+    rest[...] = rest[...] - thrice(columns, (w_high[...], w_low[...]), NT)
     put(rest, truth_hbm)
     for store in stores:
         store.wait()
 
 
-def apply_inverse(column, high, low, d_high, d_low, gathered, trailing, rest):
+def apply_inverse(column, inverse, w_high, w_low, gathered, trailing, rest):
     f32, bf16 = jnp.float32, jnp.bfloat16
     anywhere, hbm = pl.BlockSpec(memory_space=pl.ANY), pl.BlockSpec(memory_space=pltpu.HBM)
     keep = pltpu.with_memory_space_constraint
@@ -330,11 +316,10 @@
             jax.ShapeDtypeStruct((16, 320), f32),
             jax.ShapeDtypeStruct((320, 448), f32),
         ),
-        in_specs=[pl.BlockSpec(memory_space=pltpu.SMEM)] + [anywhere] * 4 + [hbm] * 3,
+        in_specs=[pl.BlockSpec(memory_space=pltpu.SMEM)] + [anywhere] * 3 + [hbm] * 3,
         out_specs=(hbm,) * 3,
         scratch_shapes=[
-            pltpu.VMEM((512, 512), bf16),
-            pltpu.VMEM((512, 512), bf16),
+            pltpu.VMEM((16, 512), f32),
             pltpu.VMEM((448, 512), bf16),
             pltpu.VMEM((448, 512), bf16),
             pltpu.VMEM((32, 40, 512), f32),
@@ -343,13 +328,13 @@
             pltpu.VMEM((896, 512), f32),
             pltpu.VMEM((512, 384), f32),
             pltpu.VMEM((16, 320), f32),
-            pltpu.SemaphoreType.DMA((8,)),
+            pltpu.SemaphoreType.DMA((7,)),
             pltpu.SemaphoreType.DMA((4,)),
         ],
         compiler_params=pltpu.CompilerParams(vmem_limit_bytes=24 * 2**20),
         cost_estimate=pl.CostEstimate(flops=4 * 10**9, bytes_accessed=10**7, transcendentals=0),
         name="apply_inverse",
-    )(column, high, low, d_high, d_low, *(keep(x, pltpu.HBM) for x in (gathered, trailing, rest)))
+    )(column, inverse, w_high, w_low, *(keep(x, pltpu.HBM) for x in (gathered, trailing, rest)))
 
 
 def per_device(diag_block, panel, trailing, truth_panel, truth_rest):
@@ -362,11 +347,11 @@
     whole = lax.all_to_all(copy_out(strip), rows, 0, 0).reshape(512, 512)
     copies, whole = lax.optimization_barrier((copy_out(panel), whole))
     dealt = lax.all_to_all(copies, rows, 0, 0)
-    high, low = invert_factor(whole)
+    inverse = invert_factor(whole)
     column = (lax.axis_index("z") * 2 + lax.axis_index("k")).astype(jnp.int32)[None]
-    d_high, d_low, factor = solve_dealt(high, low, dealt, panel)
+    w_high, w_low, factor = solve_dealt(inverse, dealt, panel)
     updated, solved, truth_updated = apply_inverse(
-        column, high, low, d_high, d_low, gathered, trailing.T, truth_rest
+        column, inverse, w_high, w_low, gathered, trailing.T, truth_rest
     )
     return factor, updated.T, solved.T, truth_updated
 

time: 105 us -> 103 us (0.981)
  waiting for transfers between devices: 19.2 us -> 17.1 us
    pallas_call x1, Pallas kernels: 2.47 us -> 4.75 us  [solve_dealt(): pl.pallas_call(dealt_kernel, out_shape=(half, half, jax.ShapeDtypeStruct(...]
    all_gather x1, waiting for transfers between devices: 4.31 us -> 2.03 us  [per_device(): gathered = lax.all_gather(packed, columns, axis=0, tiled=False)]
    pallas_call x1, Pallas kernels: 9.11 us -> 6.99 us  [apply_inverse(): pl.pallas_call(apply_kernel, out_shape=(jax.ShapeDtypeStruct((448, 896),...]
  transfers between devices with their start and end apart: 3 -> 3, of which waited for: 3 -> 3; matrix products, arithmetic and copies ran while one was open for 1% -> 1% of each run, Pallas kernels for 18% -> 20%
where the time goes in v6:
time: 103 us; the launch traced here: 102 us
  blocking collectives  29.6 us (29%)
  Pallas kernels  28.9 us (28%)
  waiting for transfers between devices  17.1 us (17%)
  between operations  14.1 us (14%)
  starting transfers between devices  11.1 us (11%)
  local copies, waits for them, and re-layouts  1.5 us (1%)
    all_to_all x1, blocking collectives, per_device(): pieces = lax.all_to_all(small, columns, 0, 0)  29.6 us
    all_to_all x1, waiting for transfers between devices, per_device(): whole = lax.all_to_all(copy_out(strip), rows, 0, 0).reshape(512, 512)  13.9 us
    pallas_call x1, Pallas kernels, invert_factor(): pl.pallas_call(invert_kernel, out_shape=jax.ShapeDtypeStruct((n, n), jnp....  13.5 us
    pallas_call x1, Pallas kernels, apply_inverse(): pl.pallas_call(apply_kernel, out_shape=(jax.ShapeDtypeStruct((448, 896),...  6.99 us
    all_to_all x1, starting transfers between devices, per_device(): whole = lax.all_to_all(copy_out(strip), rows, 0, 0).reshape(512, 512)  6.76 us
    pallas_call x1, Pallas kernels, solve_dealt(): pl.pallas_call(dealt_kernel, out_shape=(half, half, jax.ShapeDtypeStruct(...  4.75 us
    all_to_all x1, starting transfers between devices, per_device(): dealt = lax.all_to_all(copies, rows, 0, 0)  4.31 us
    pallas_call x2, Pallas kernels, copy_out(): pl.pallas_call(copy_kernel, out_shape=jax.ShapeDtypeStruct((16,) + strip....  2.22 us
  transfers between devices with their start and end apart: 3, of which 3 were waited for; matrix products, arithmetic and copies ran while one was open for 1% of the time, Pallas kernels for 20%

profile of v6, /device:TPU:1, one launch (start us, length us, event | category | flops | bytes accessed | tf_op | source)
XLA Modules:
  0.0 102.3 jit_solution(6186749156889353502)
XLA Ops:
  7.2 0.0 all-gather.3.cloned.1.call-start
  7.2 1.5 %pack.1 = f32[40,512]{1,0:T(8,128)} custom-call(f32[28,512]{1,0:T(8,128)} %panel_hbm.3, f32[16,320]{1,0:T(8,128)} %bitcast.14), custom_call_target="tpu_custom_call" | custom-call | tf_op jit(solution)/shard_map/pack/pallas_call | solution.py:153
  8.7 0.0 all-gather.3.cloned.1.call-update
  8.7 0.8 copy.11
  9.5 0.1 broadcast_in_dim.10
  9.6 29.6 %all_to_all.15 = f32[32,4,128]{2,1,0:T(4,128)S(1)} all-to-all(f32[32,4,128]{2,1,0:T(4,128)S(1)} %broadcast_in_dim.11), channel_id=1, replica_groups=mesh['x'=4,'y'=4,'z'=16,'k'=2] {'z','k'}, dimensions={0} | all-to-all | bytes 131072 | tf_op jit(solution)/shard_map/all_to_all | solution.py:345
  39.2 0.1 copy.12
  39.3 0.2 copy.13
  39.5 0.3 reshape.20.strip_ref
  39.8 0.0 copy-start
  39.8 1.1 %copy_out.3 = f32[16,32,512]{2,1,0:T(8,128)} custom-call(f32[32,512]{1,0:T(8,128)S(1)} %reshape.20.strip_ref), custom_call_target="tpu_custom_call" | custom-call | tf_op jit(solution)/shard_map/copy_out/pallas_call | solution.py:178
  40.9 6.8 %all-to-all-start.1 = ((f32[16,32,512]{2,1,0:T(8,128)}), f32[16,32,512]{2,1,0:T(8,128)S(1)}, u32[]{:S(2)}, u32[]{:S(2)}) async-start(f32[16,32,512]{2,1,0:T(8,128)} %copy_out.3), calls=%async_computation.1 | async-start | bytes 2097152 | tf_op jit(solution)/shard_map/all_to_all | solution.py:347
  47.7 0.0 copy-done
  47.7 1.1 %copy_out.2 = f32[16,28,512]{2,1,0:T(8,128)} custom-call(f32[28,512]{1,0:T(8,128)S(1)} %copy-done), custom_call_target="tpu_custom_call" | custom-call | tf_op jit(solution)/shard_map/copy_out/pallas_call | solution.py:178
  48.8 13.9 %all-to-all-done.1 = f32[16,32,512]{2,1,0:T(8,128)S(1)} async-done(((f32[16,32,512]{2,1,0:T(8,128)}), f32[16,32,512]{2,1,0:T(8,128)S(1)}, u32[]{:S(2)}, u32[]{:S(2)}) %all-to-all-start.1) | async-done | bytes 1048608 | tf_op jit(solution)/shard_map/all_to_all | solution.py:347
  62.7 4.3 %all-to-all-start.2 = ((f32[16,28,512]{2,1,0:T(8,128)}), f32[16,28,512]{2,1,0:T(8,128)S(1)}, u32[]{:S(2)}, u32[]{:S(2)}) async-start(f32[16,28,512]{2,1,0:T(8,128)} %copy_out.2), calls=%async_computation.2 | async-start | bytes 2097152 | tf_op jit(solution)/shard_map/all_to_all | solution.py:349
  67.0 13.5 %invert_factor.1.inverse_any = f32[512,512]{1,0:T(8,128)S(1)} custom-call(f32[512,512]{1,0:T(8,128)S(1)} %bitcast.12), custom_call_target="tpu_custom_call" | custom-call | flops 10000000000 | bytes 2000000 | tf_op jit(solution)/shard_map/invert_factor/pallas_call | solution.py:113
  80.5 1.1 %all-to-all-done.2.dealt_any = f32[16,28,512]{2,1,0:T(8,128)S(1)} async-done(((f32[16,28,512]{2,1,0:T(8,128)}), f32[16,28,512]{2,1,0:T(8,128)S(1)}, u32[]{:S(2)}, u32[]{:S(2)}) %all-to-all-start.2) | async-done | bytes 917536 | tf_op jit(solution)/shard_map/all_to_all | solution.py:349
  81.6 4.8 %solve_dealt.1 = (bf16[448,512]{1,0:T(8,128)(2,1)S(1)}, bf16[448,512]{1,0:T(8,128)(2,1)S(1)}, f32[28,512]{1,0:T(8,128)}) custom-call(f32[512,512]{1,0:T(8,128)S(1)} %invert_factor.1.inverse_any, f32[16,28,512]{2,1,0:T(8,128)S(1)} %all-to-all-done.2.dealt_any, f32[28,512]{1,0:T(8,128)} %panel_hbm.3), custom_call_target="tpu_custom_call" | custom-call | flops 1000000000 | bytes 2000000 | tf_op jit(solution)/shard_map/solve_dealt/pallas_call | solution.py:231
  86.4 2.0 %all-gather.3.cloned.1.call-done = f32[1280,512]{1,0:T(8,128)} async-done(((f32[40,512]{1,0:T(8,128)}), f32[1280,512]{1,0:T(8,128)}) %all-gather.3.cloned.1.call-update) | async-done | bytes 2621456 | tf_op jit(solution)/shard_map/all_gather | solution.py:343
  88.4 7.0 %apply_inverse.1 = (f32[448,896]{1,0:T(8,128)}, f32[16,320]{1,0:T(8,128)}, f32[320,448]{1,0:T(8,128)}) custom-call(s32[1]{0:T(128)} %bitcast.3.col_ref, f32[512,512]{1,0:T(8,128)S(1)} %invert_factor.1.inverse_any, bf16[448,512]{1,0:T(8,128)(2,1)S(1)} %get-tuple-element.15.w_high_any, bf16[448,512]{1,0:T(8,128)(2,1)S(1)} %get-tuple-element.16.w_low_any, ...), custom_call_target="tpu_custom_call" | custom-call | flops 4000000000 | bytes 10000000 | tf_op jit(solution)/shard_map/apply_inverse/pallas_call | solution.py:312
  (1 shorter events, 0.0 us)
Async XLA Ops:
  7.2 81.3 %all-gather.3.cloned.1.call-start = ((), (), s32[]{:S(2)}) async-start(), calls=%async_computation.3 | async-start | bytes 2703360 | tf_op jit(solution)/shard_map/all_gather | solution.py:343
  39.8 7.9 %copy-start = (f32[28,512]{1,0:T(8,128)S(1)}, f32[28,512]{1,0:T(8,128)}, u32[]{:S(2)}) copy-start(f32[28,512]{1,0:T(8,128)} %panel_hbm.3) | copy-start | bytes 172036
  40.9 21.8 %all-to-all-start.1 = ((f32[16,32,512]{2,1,0:T(8,128)}), f32[16,32,512]{2,1,0:T(8,128)S(1)}, u32[]{:S(2)}, u32[]{:S(2)}) async-start(f32[16,32,512]{2,1,0:T(8,128)} %copy_out.3), calls=%async_computation.1 | async-start | bytes 2097152 | tf_op jit(solution)/shard_map/all_to_all | solution.py:347
  62.7 18.9 %all-to-all-start.2 = ((f32[16,28,512]{2,1,0:T(8,128)}), f32[16,28,512]{2,1,0:T(8,128)S(1)}, u32[]{:S(2)}, u32[]{:S(2)}) async-start(f32[16,28,512]{2,1,0:T(8,128)} %copy_out.2), calls=%async_computation.2 | async-start | bytes 2097152 | tf_op jit(solution)/shard_map/all_to_all | solution.py:349
Sparse Core Ops, SparseCore 0:
  10.7 77.7 all-gather.2

commit v7 on v6

--- a/solution.py
+++ b/solution.py
@@ -254,18 +254,17 @@
     own, w_high, w_low, gathered, trailing, rest, stack, truth, solved, sem, out_sem,
 ):
     at = pl.ds(pl.multiple_of(col_ref[0] * 16, 16), 16)
+    pieces = ((0, 10), (10, 19), (19, 28), (28, 32))
     loads = [
         pltpu.make_async_copy(src, dst, sem.at[i])
         for i, (src, dst) in enumerate(
-            [
-                (gathered_hbm.at[0:19], gathered.at[0:19]), (w_high_any, w_high), (w_low_any, w_low),
-                (trailing_hbm, trailing), (gathered_hbm.at[19:32], gathered.at[19:32]),
+            [(gathered_hbm.at[a:b], gathered.at[a:b]) for a, b in pieces]
+            + [
+                (w_high_any, w_high), (w_low_any, w_low), (trailing_hbm, trailing),
                 (inverse_any.at[at], own), (rest_hbm, rest),
             ]
         )
     ]
-    for load in loads:
-        load.start()
     stores = []
 
     def unpack(first, last):
@@ -281,26 +280,39 @@
         store.start()
         stores.append(store)
 
-    def update(first, last):
-        rows = halves(stack[first:last, :])
-        trailing[:, first:last] = trailing[:, first:last] - thrice((w_high[...], w_low[...]), rows, NT)
+    def product(first, last):
+        return thrice((w_high[...], w_low[...]), halves(stack[first:last, :]), NT)
+
+    def finish(first, last, value):
+        trailing[:, first:last] = trailing[:, first:last] - value
         put(trailing.at[:, first:last], updated_hbm.at[:, first:last])
 
+    for i in (0, 4, 5, 1):
+        loads[i].start()
     loads[0].wait()
-    unpack(0, 19)
-    for load in loads[1:4]:
-        load.wait()
-    update(0, 512)
-    loads[4].wait()
-    unpack(19, 32)
-    update(512, 896)
+    for i in (6, 2, 3, 7, 8):
+        loads[i].start()
+    unpack(0, 10)
+    for i in (4, 5, 1):
+        loads[i].wait()
+    unpack(10, 19)
+    value = product(0, 256)
+    for i in (6, 2):
+        loads[i].wait()
+    finish(0, 256, value)
+    unpack(19, 28)
+    value = product(256, 512)
+    for i in (3, 7, 8):
+        loads[i].wait()
+    finish(256, 512, value)
+    unpack(28, 32)
+    finish(512, 768, product(512, 768))
     columns = halves(truth[...].T[0:320, :])
-    loads[5].wait()
+    rest[...] = rest[...] - thrice(columns, (w_high[...], w_low[...]), NT)
+    put(rest, truth_hbm)
     solved[...] = thrice(halves(own[...]), columns, NT)
     put(solved, solved_hbm)
-    loads[6].wait()
-    rest[...] = rest[...] - thrice(columns, (w_high[...], w_low[...]), NT)
-    put(rest, truth_hbm)
+    finish(768, 896, product(768, 896))
     for store in stores:
         store.wait()
 
@@ -328,8 +340,8 @@
             pltpu.VMEM((896, 512), f32),
             pltpu.VMEM((512, 384), f32),
             pltpu.VMEM((16, 320), f32),
-            pltpu.SemaphoreType.DMA((7,)),
-            pltpu.SemaphoreType.DMA((4,)),
+            pltpu.SemaphoreType.DMA((9,)),
+            pltpu.SemaphoreType.DMA((6,)),
         ],
         compiler_params=pltpu.CompilerParams(vmem_limit_bytes=24 * 2**20),
         cost_estimate=pl.CostEstimate(flops=4 * 10**9, bytes_accessed=10**7, transcendentals=0),

time: 103 us -> 102 us (level)
  no operation moved by 1% of the time
where the time goes in v7:
time: 102 us
  blocking collectives  29.6 us (29%)
  Pallas kernels  28.2 us (28%)
  waiting for transfers between devices  17.1 us (17%)
  between operations  14.1 us (14%)
  starting transfers between devices  11.1 us (11%)
  local copies, waits for them, and re-layouts  1.5 us (1%)
    all_to_all x1, blocking collectives, per_device(): pieces = lax.all_to_all(small, columns, 0, 0)  29.6 us
    all_to_all x1, waiting for transfers between devices, per_device(): whole = lax.all_to_all(copy_out(strip), rows, 0, 0).reshape(512, 512)  13.9 us
    pallas_call x1, Pallas kernels, invert_factor(): pl.pallas_call(invert_kernel, out_shape=jax.ShapeDtypeStruct((n, n), jnp....  13.5 us
    all_to_all x1, starting transfers between devices, per_device(): whole = lax.all_to_all(copy_out(strip), rows, 0, 0).reshape(512, 512)  6.76 us
    pallas_call x1, Pallas kernels, apply_inverse(): pl.pallas_call(apply_kernel, out_shape=(jax.ShapeDtypeStruct((448, 896),...  6.28 us
    pallas_call x1, Pallas kernels, solve_dealt(): pl.pallas_call(dealt_kernel, out_shape=(half, half, jax.ShapeDtypeStruct(...  4.75 us
    all_to_all x1, starting transfers between devices, per_device(): dealt = lax.all_to_all(copies, rows, 0, 0)  4.31 us
    pallas_call x2, Pallas kernels, copy_out(): pl.pallas_call(copy_kernel, out_shape=jax.ShapeDtypeStruct((16,) + strip....  2.22 us
  transfers between devices with their start and end apart: 3, of which 3 were waited for; matrix products, arithmetic and copies ran while one was open for 1% of the time, Pallas kernels for 20%

profile of v7, /device:TPU:1, one launch (start us, length us, event | category | flops | bytes accessed | tf_op | source)
XLA Modules:
  0.0 101.6 jit_solution(10079578985974567176)
XLA Ops:
  7.2 0.0 all-gather.3.cloned.1.call-start
  7.2 1.5 %pack.1 = f32[40,512]{1,0:T(8,128)} custom-call(f32[28,512]{1,0:T(8,128)} %panel_hbm.3, f32[16,320]{1,0:T(8,128)} %bitcast.14), custom_call_target="tpu_custom_call" | custom-call | tf_op jit(solution)/shard_map/pack/pallas_call | solution.py:153
  8.7 0.0 all-gather.3.cloned.1.call-update
  8.7 0.8 copy.11
  9.5 0.1 broadcast_in_dim.10
  9.6 29.6 %all_to_all.15 = f32[32,4,128]{2,1,0:T(4,128)S(1)} all-to-all(f32[32,4,128]{2,1,0:T(4,128)S(1)} %broadcast_in_dim.11), channel_id=1, replica_groups=mesh['x'=4,'y'=4,'z'=16,'k'=2] {'z','k'}, dimensions={0} | all-to-all | bytes 131072 | tf_op jit(solution)/shard_map/all_to_all | solution.py:357
  39.2 0.1 copy.12
  39.3 0.2 copy.13
  39.5 0.3 reshape.20.strip_ref
  39.8 0.0 copy-start
  39.8 1.1 %copy_out.3 = f32[16,32,512]{2,1,0:T(8,128)} custom-call(f32[32,512]{1,0:T(8,128)S(1)} %reshape.20.strip_ref), custom_call_target="tpu_custom_call" | custom-call | tf_op jit(solution)/shard_map/copy_out/pallas_call | solution.py:178
  40.9 6.8 %all-to-all-start.1 = ((f32[16,32,512]{2,1,0:T(8,128)}), f32[16,32,512]{2,1,0:T(8,128)S(1)}, u32[]{:S(2)}, u32[]{:S(2)}) async-start(f32[16,32,512]{2,1,0:T(8,128)} %copy_out.3), calls=%async_computation.1 | async-start | bytes 2097152 | tf_op jit(solution)/shard_map/all_to_all | solution.py:359
  47.7 0.0 copy-done
  47.7 1.1 %copy_out.2 = f32[16,28,512]{2,1,0:T(8,128)} custom-call(f32[28,512]{1,0:T(8,128)S(1)} %copy-done), custom_call_target="tpu_custom_call" | custom-call | tf_op jit(solution)/shard_map/copy_out/pallas_call | solution.py:178
  48.8 13.9 %all-to-all-done.1 = f32[16,32,512]{2,1,0:T(8,128)S(1)} async-done(((f32[16,32,512]{2,1,0:T(8,128)}), f32[16,32,512]{2,1,0:T(8,128)S(1)}, u32[]{:S(2)}, u32[]{:S(2)}) %all-to-all-start.1) | async-done | bytes 1048608 | tf_op jit(solution)/shard_map/all_to_all | solution.py:359
  62.7 4.3 %all-to-all-start.2 = ((f32[16,28,512]{2,1,0:T(8,128)}), f32[16,28,512]{2,1,0:T(8,128)S(1)}, u32[]{:S(2)}, u32[]{:S(2)}) async-start(f32[16,28,512]{2,1,0:T(8,128)} %copy_out.2), calls=%async_computation.2 | async-start | bytes 2097152 | tf_op jit(solution)/shard_map/all_to_all | solution.py:361
  67.0 13.5 %invert_factor.1.inverse_any = f32[512,512]{1,0:T(8,128)S(1)} custom-call(f32[512,512]{1,0:T(8,128)S(1)} %bitcast.12), custom_call_target="tpu_custom_call" | custom-call | flops 10000000000 | bytes 2000000 | tf_op jit(solution)/shard_map/invert_factor/pallas_call | solution.py:113
  80.5 1.1 %all-to-all-done.2.dealt_any = f32[16,28,512]{2,1,0:T(8,128)S(1)} async-done(((f32[16,28,512]{2,1,0:T(8,128)}), f32[16,28,512]{2,1,0:T(8,128)S(1)}, u32[]{:S(2)}, u32[]{:S(2)}) %all-to-all-start.2) | async-done | bytes 917536 | tf_op jit(solution)/shard_map/all_to_all | solution.py:361
  81.6 4.8 %solve_dealt.1 = (bf16[448,512]{1,0:T(8,128)(2,1)S(1)}, bf16[448,512]{1,0:T(8,128)(2,1)S(1)}, f32[28,512]{1,0:T(8,128)}) custom-call(f32[512,512]{1,0:T(8,128)S(1)} %invert_factor.1.inverse_any, f32[16,28,512]{2,1,0:T(8,128)S(1)} %all-to-all-done.2.dealt_any, f32[28,512]{1,0:T(8,128)} %panel_hbm.3), custom_call_target="tpu_custom_call" | custom-call | flops 1000000000 | bytes 2000000 | tf_op jit(solution)/shard_map/solve_dealt/pallas_call | solution.py:231
  86.4 2.0 %all-gather.3.cloned.1.call-done = f32[1280,512]{1,0:T(8,128)} async-done(((f32[40,512]{1,0:T(8,128)}), f32[1280,512]{1,0:T(8,128)}) %all-gather.3.cloned.1.call-update) | async-done | bytes 2621456 | tf_op jit(solution)/shard_map/all_gather | solution.py:355
  88.4 6.3 %apply_inverse.1 = (f32[448,896]{1,0:T(8,128)}, f32[16,320]{1,0:T(8,128)}, f32[320,448]{1,0:T(8,128)}) custom-call(s32[1]{0:T(128)} %bitcast.3.col_ref, f32[512,512]{1,0:T(8,128)S(1)} %invert_factor.1.inverse_any, bf16[448,512]{1,0:T(8,128)(2,1)S(1)} %get-tuple-element.15.w_high_any, bf16[448,512]{1,0:T(8,128)(2,1)S(1)} %get-tuple-element.16.w_low_any, ...), custom_call_target="tpu_custom_call" | custom-call | flops 4000000000 | bytes 10000000 | tf_op jit(solution)/shard_map/apply_inverse/pallas_call | solution.py:324
  (1 shorter events, 0.0 us)
Async XLA Ops:
  7.2 81.3 %all-gather.3.cloned.1.call-start = ((), (), s32[]{:S(2)}) async-start(), calls=%async_computation.3 | async-start | bytes 2703360 | tf_op jit(solution)/shard_map/all_gather | solution.py:355
  39.8 7.9 %copy-start = (f32[28,512]{1,0:T(8,128)S(1)}, f32[28,512]{1,0:T(8,128)}, u32[]{:S(2)}) copy-start(f32[28,512]{1,0:T(8,128)} %panel_hbm.3) | copy-start | bytes 172036
  40.9 21.8 %all-to-all-start.1 = ((f32[16,32,512]{2,1,0:T(8,128)}), f32[16,32,512]{2,1,0:T(8,128)S(1)}, u32[]{:S(2)}, u32[]{:S(2)}) async-start(f32[16,32,512]{2,1,0:T(8,128)} %copy_out.3), calls=%async_computation.1 | async-start | bytes 2097152 | tf_op jit(solution)/shard_map/all_to_all | solution.py:359
  62.7 18.9 %all-to-all-start.2 = ((f32[16,28,512]{2,1,0:T(8,128)}), f32[16,28,512]{2,1,0:T(8,128)S(1)}, u32[]{:S(2)}, u32[]{:S(2)}) async-start(f32[16,28,512]{2,1,0:T(8,128)} %copy_out.2), calls=%async_computation.2 | async-start | bytes 2097152 | tf_op jit(solution)/shard_map/all_to_all | solution.py:361
Sparse Core Ops, SparseCore 0:
  10.7 77.7 all-gather.2

commit v8 on v7

--- a/solution.py
+++ b/solution.py
@@ -191,7 +191,7 @@
     return dot(a[0], b[0]) + dot(a[0], b[1]) + dot(a[1], b[0])
 
 
-def dealt_kernel(inverse_any, dealt_any, panel_hbm, w_high_any, w_low_any, factor_hbm, inverse, dealt, stack, w_high, w_low, factor, sem):
+def dealt_kernel(inverse_any, dealt_any, panel_hbm, w_high, w_low, factor_hbm, inverse, dealt, stack, factor, sem):
     loads = [
         pltpu.make_async_copy(src, dst, sem.at[i])
         for i, (src, dst) in enumerate([(dealt_any, dealt), (panel_hbm, factor), (inverse_any, inverse)])
@@ -214,33 +214,27 @@
     w_right = dot(right[:448], inverse[256:, 256:], NN)
     w_high[:, :256], w_low[:, :256] = halves(w_left)
     w_high[:, 256:], w_low[:, 256:] = halves(w_right)
-    stores = [
-        pltpu.make_async_copy(src, dst, sem.at[3 + i])
-        for i, (src, dst) in enumerate([(factor, factor_hbm), (w_high, w_high_any), (w_low, w_low_any)])
-    ]
-    for store in stores:
-        store.start()
-    for store in stores:
-        store.wait()
+    store = pltpu.make_async_copy(factor, factor_hbm, sem.at[3])
+    store.start()
+    store.wait()
 
 
 def solve_dealt(inverse, dealt, panel):
     f32, bf16 = jnp.float32, jnp.bfloat16
     anywhere, hbm = pl.BlockSpec(memory_space=pl.ANY), pl.BlockSpec(memory_space=pltpu.HBM)
-    half = jax.ShapeDtypeStruct((448, 512), bf16)
+    half = pltpu.VMEM((448, 512), bf16)
+    vmem = pl.BlockSpec(memory_space=pltpu.VMEM)
     return pl.pallas_call(
         dealt_kernel,
         out_shape=(half, half, jax.ShapeDtypeStruct((28, 512), f32)),
         in_specs=[anywhere] * 2 + [hbm],
-        out_specs=(anywhere, anywhere, hbm),
+        out_specs=(vmem, vmem, hbm),
         scratch_shapes=[
             pltpu.VMEM((512, 512), f32),
             pltpu.VMEM((16, 28, 512), f32),
             pltpu.VMEM((480, 512), f32),
-            pltpu.VMEM((448, 512), bf16),
-            pltpu.VMEM((448, 512), bf16),
             pltpu.VMEM((28, 512), f32),
-            pltpu.SemaphoreType.DMA((6,)),
+            pltpu.SemaphoreType.DMA((4,)),
         ],
         compiler_params=pltpu.CompilerParams(vmem_limit_bytes=16 * 2**20),
         cost_estimate=pl.CostEstimate(flops=10**9, bytes_accessed=2 * 10**6, transcendentals=0),
@@ -249,9 +243,9 @@
 
 
 def apply_kernel(
-    col_ref, inverse_any, w_high_any, w_low_any, gathered_hbm, trailing_hbm, rest_hbm,
+    col_ref, inverse_any, w_high, w_low, gathered_hbm, trailing_hbm, rest_hbm,
     updated_hbm, solved_hbm, truth_hbm,
-    own, w_high, w_low, gathered, trailing, rest, stack, truth, solved, sem, out_sem,
+    own, gathered, trailing, rest, stack, truth, solved, sem, out_sem,
 ):
     at = pl.ds(pl.multiple_of(col_ref[0] * 16, 16), 16)
     pieces = ((0, 10), (10, 19), (19, 28), (28, 32))
@@ -260,7 +254,7 @@
         for i, (src, dst) in enumerate(
             [(gathered_hbm.at[a:b], gathered.at[a:b]) for a, b in pieces]
             + [
-                (w_high_any, w_high), (w_low_any, w_low), (trailing_hbm, trailing),
+                (trailing_hbm, trailing),
                 (inverse_any.at[at], own), (rest_hbm, rest),
             ]
         )
@@ -281,38 +275,45 @@
         stores.append(store)
 
     def product(first, last):
-        return thrice((w_high[...], w_low[...]), halves(stack[first:last, :]), NT)
+        high, low = halves(stack[first:last, :])
+        dot = lambda p, q: lax.dot_general(p, q, NT, preferred_element_type=jnp.float32)
+        both = dot(jnp.concatenate([w_high[...], w_low[...]], 0), high)
+        return both[:448] + both[448:] + dot(w_high[...], low)
 
     def finish(first, last, value):
         trailing[:, first:last] = trailing[:, first:last] - value
+
+    def send(first, last):
         put(trailing.at[:, first:last], updated_hbm.at[:, first:last])
 
-    for i in (0, 4, 5, 1):
+    for i in (0, 1):
         loads[i].start()
     loads[0].wait()
-    for i in (6, 2, 3, 7, 8):
+    for i in (4, 2, 3, 5, 6):
         loads[i].start()
     unpack(0, 10)
-    for i in (4, 5, 1):
-        loads[i].wait()
+    loads[1].wait()
+    value = product(0, 256)
     unpack(10, 19)
-    value = product(0, 256)
-    for i in (6, 2):
+    for i in (4, 2, 3, 5, 6):
         loads[i].wait()
     finish(0, 256, value)
-    unpack(19, 28)
     value = product(256, 512)
-    for i in (3, 7, 8):
-        loads[i].wait()
+    unpack(19, 32)
+    columns = halves(truth[...].T[0:320, :])
     finish(256, 512, value)
-    unpack(28, 32)
-    finish(512, 768, product(512, 768))
-    columns = halves(truth[...].T[0:320, :])
+    value = product(512, 768)
+    send(0, 256)
+    send(256, 512)
+    finish(512, 768, value)
     rest[...] = rest[...] - thrice(columns, (w_high[...], w_low[...]), NT)
+    solved[...] = thrice(halves(own[...]), columns, NT)
+    value = product(768, 896)
+    send(512, 768)
     put(rest, truth_hbm)
-    solved[...] = thrice(halves(own[...]), columns, NT)
     put(solved, solved_hbm)
-    finish(768, 896, product(768, 896))
+    finish(768, 896, value)
+    send(768, 896)
     for store in stores:
         store.wait()
 
@@ -328,25 +329,23 @@
             jax.ShapeDtypeStruct((16, 320), f32),
             jax.ShapeDtypeStruct((320, 448), f32),
         ),
-        in_specs=[pl.BlockSpec(memory_space=pltpu.SMEM)] + [anywhere] * 3 + [hbm] * 3,
+        in_specs=[pl.BlockSpec(memory_space=pltpu.SMEM), anywhere] + [pl.BlockSpec(memory_space=pltpu.VMEM)] * 2 + [hbm] * 3,
         out_specs=(hbm,) * 3,
         scratch_shapes=[
             pltpu.VMEM((16, 512), f32),
-            pltpu.VMEM((448, 512), bf16),
-            pltpu.VMEM((448, 512), bf16),
             pltpu.VMEM((32, 40, 512), f32),
             pltpu.VMEM((448, 896), f32),
             pltpu.VMEM((320, 448), f32),
             pltpu.VMEM((896, 512), f32),
             pltpu.VMEM((512, 384), f32),
             pltpu.VMEM((16, 320), f32),
-            pltpu.SemaphoreType.DMA((9,)),
+            pltpu.SemaphoreType.DMA((7,)),
             pltpu.SemaphoreType.DMA((6,)),
         ],
         compiler_params=pltpu.CompilerParams(vmem_limit_bytes=24 * 2**20),
         cost_estimate=pl.CostEstimate(flops=4 * 10**9, bytes_accessed=10**7, transcendentals=0),
         name="apply_inverse",
-    )(column, inverse, w_high, w_low, *(keep(x, pltpu.HBM) for x in (gathered, trailing, rest)))
+    )(column, inverse, keep(w_high, pltpu.VMEM), keep(w_low, pltpu.VMEM), *(keep(x, pltpu.HBM) for x in (gathered, trailing, rest)))
 
 
 def per_device(diag_block, panel, trailing, truth_panel, truth_rest):

time: 102 us -> 102 us (level)
  no operation moved by 1% of the time
where the time goes in v8:
time: 102 us
  blocking collectives  29.6 us (29%)
  Pallas kernels  27.8 us (27%)
  waiting for transfers between devices  17.6 us (17%)
  between operations  14.1 us (14%)
  starting transfers between devices  11.1 us (11%)
  local copies, waits for them, and re-layouts  1.5 us (1%)
    all_to_all x1, blocking collectives, per_device(): pieces = lax.all_to_all(small, columns, 0, 0)  29.6 us
    all_to_all x1, waiting for transfers between devices, per_device(): whole = lax.all_to_all(copy_out(strip), rows, 0, 0).reshape(512, 512)  13.9 us
    pallas_call x1, Pallas kernels, invert_factor(): pl.pallas_call(invert_kernel, out_shape=jax.ShapeDtypeStruct((n, n), jnp....  13.5 us
    all_to_all x1, starting transfers between devices, per_device(): whole = lax.all_to_all(copy_out(strip), rows, 0, 0).reshape(512, 512)  6.76 us
    pallas_call x1, Pallas kernels, apply_inverse(): pl.pallas_call(apply_kernel, out_shape=(jax.ShapeDtypeStruct((448, 896),...  6.37 us
    all_to_all x1, starting transfers between devices, per_device(): dealt = lax.all_to_all(copies, rows, 0, 0)  4.31 us
    pallas_call x1, Pallas kernels, solve_dealt(): pl.pallas_call(dealt_kernel, out_shape=(half, half, jax.ShapeDtypeStruct(...  4.2 us
    all_gather x1, waiting for transfers between devices, per_device(): gathered = lax.all_gather(packed, columns, axis=0, tiled=False)  2.59 us
  transfers between devices with their start and end apart: 3, of which 3 were waited for; matrix products, arithmetic and copies ran while one was open for 1% of the time, Pallas kernels for 20%

profile of v8, /device:TPU:1, one launch (start us, length us, event | category | flops | bytes accessed | tf_op | source)
XLA Modules:
  0.0 101.7 jit_solution(17398365158264959944)
XLA Ops:
  7.2 0.0 all-gather.3.cloned.1.call-start
  7.2 1.5 %pack.1 = f32[40,512]{1,0:T(8,128)} custom-call(f32[28,512]{1,0:T(8,128)} %panel_hbm.3, f32[16,320]{1,0:T(8,128)} %bitcast.14), custom_call_target="tpu_custom_call" | custom-call | tf_op jit(solution)/shard_map/pack/pallas_call | solution.py:153
  8.7 0.0 all-gather.3.cloned.1.call-update
  8.7 0.8 copy.11
  9.5 0.1 broadcast_in_dim.10
  9.6 29.6 %all_to_all.15 = f32[32,4,128]{2,1,0:T(4,128)S(1)} all-to-all(f32[32,4,128]{2,1,0:T(4,128)S(1)} %broadcast_in_dim.11), channel_id=1, replica_groups=mesh['x'=4,'y'=4,'z'=16,'k'=2] {'z','k'}, dimensions={0} | all-to-all | bytes 131072 | tf_op jit(solution)/shard_map/all_to_all | solution.py:356
  39.2 0.1 copy.12
  39.3 0.2 copy.13
  39.5 0.3 reshape.20.strip_ref
  39.8 0.0 copy-start
  39.8 1.1 %copy_out.3 = f32[16,32,512]{2,1,0:T(8,128)} custom-call(f32[32,512]{1,0:T(8,128)S(1)} %reshape.20.strip_ref), custom_call_target="tpu_custom_call" | custom-call | tf_op jit(solution)/shard_map/copy_out/pallas_call | solution.py:178
  40.9 6.8 %all-to-all-start.1 = ((f32[16,32,512]{2,1,0:T(8,128)}), f32[16,32,512]{2,1,0:T(8,128)S(1)}, u32[]{:S(2)}, u32[]{:S(2)}) async-start(f32[16,32,512]{2,1,0:T(8,128)} %copy_out.3), calls=%async_computation.1 | async-start | bytes 2097152 | tf_op jit(solution)/shard_map/all_to_all | solution.py:358
  47.7 0.0 copy-done
  47.7 1.1 %copy_out.2 = f32[16,28,512]{2,1,0:T(8,128)} custom-call(f32[28,512]{1,0:T(8,128)S(1)} %copy-done), custom_call_target="tpu_custom_call" | custom-call | tf_op jit(solution)/shard_map/copy_out/pallas_call | solution.py:178
  48.8 13.9 %all-to-all-done.1 = f32[16,32,512]{2,1,0:T(8,128)S(1)} async-done(((f32[16,32,512]{2,1,0:T(8,128)}), f32[16,32,512]{2,1,0:T(8,128)S(1)}, u32[]{:S(2)}, u32[]{:S(2)}) %all-to-all-start.1) | async-done | bytes 1048608 | tf_op jit(solution)/shard_map/all_to_all | solution.py:358
  62.7 4.3 %all-to-all-start.2 = ((f32[16,28,512]{2,1,0:T(8,128)}), f32[16,28,512]{2,1,0:T(8,128)S(1)}, u32[]{:S(2)}, u32[]{:S(2)}) async-start(f32[16,28,512]{2,1,0:T(8,128)} %copy_out.2), calls=%async_computation.2 | async-start | bytes 2097152 | tf_op jit(solution)/shard_map/all_to_all | solution.py:360
  67.0 13.5 %invert_factor.1.inverse_any = f32[512,512]{1,0:T(8,128)S(1)} custom-call(f32[512,512]{1,0:T(8,128)S(1)} %bitcast.12), custom_call_target="tpu_custom_call" | custom-call | flops 10000000000 | bytes 2000000 | tf_op jit(solution)/shard_map/invert_factor/pallas_call | solution.py:113
  80.5 1.1 %all-to-all-done.2.dealt_any = f32[16,28,512]{2,1,0:T(8,128)S(1)} async-done(((f32[16,28,512]{2,1,0:T(8,128)}), f32[16,28,512]{2,1,0:T(8,128)S(1)}, u32[]{:S(2)}, u32[]{:S(2)}) %all-to-all-start.2) | async-done | bytes 917536 | tf_op jit(solution)/shard_map/all_to_all | solution.py:360
  81.6 4.2 %solve_dealt.1 = (bf16[448,512]{1,0:T(8,128)(2,1)S(1)}, bf16[448,512]{1,0:T(8,128)(2,1)S(1)}, f32[28,512]{1,0:T(8,128)}) custom-call(f32[512,512]{1,0:T(8,128)S(1)} %invert_factor.1.inverse_any, f32[16,28,512]{2,1,0:T(8,128)S(1)} %all-to-all-done.2.dealt_any, f32[28,512]{1,0:T(8,128)} %panel_hbm.3), custom_call_target="tpu_custom_call" | custom-call | flops 1000000000 | bytes 2000000 | tf_op jit(solution)/shard_map/solve_dealt/pallas_call | solution.py:227
  85.8 2.6 %all-gather.3.cloned.1.call-done = f32[1280,512]{1,0:T(8,128)} async-done(((f32[40,512]{1,0:T(8,128)}), f32[1280,512]{1,0:T(8,128)}) %all-gather.3.cloned.1.call-update) | async-done | bytes 2621456 | tf_op jit(solution)/shard_map/all_gather | solution.py:354
  88.4 6.4 %apply_inverse.1 = (f32[448,896]{1,0:T(8,128)}, f32[16,320]{1,0:T(8,128)}, f32[320,448]{1,0:T(8,128)}) custom-call(s32[1]{0:T(128)} %bitcast.3.col_ref, f32[512,512]{1,0:T(8,128)S(1)} %invert_factor.1.inverse_any, bf16[448,512]{1,0:T(8,128)(2,1)S(1)} %get-tuple-element.15.w_high, bf16[448,512]{1,0:T(8,128)(2,1)S(1)} %get-tuple-element.16.w_low, ...), custom_call_target="tpu_custom_call" | custom-call | flops 4000000000 | bytes 10000000 | tf_op jit(solution)/shard_map/apply_inverse/pallas_call | solution.py:325
  (1 shorter events, 0.0 us)
Async XLA Ops:
  7.2 81.3 %all-gather.3.cloned.1.call-start = ((), (), s32[]{:S(2)}) async-start(), calls=%async_computation.3 | async-start | bytes 2703360 | tf_op jit(solution)/shard_map/all_gather | solution.py:354
  39.8 7.9 %copy-start = (f32[28,512]{1,0:T(8,128)S(1)}, f32[28,512]{1,0:T(8,128)}, u32[]{:S(2)}) copy-start(f32[28,512]{1,0:T(8,128)} %panel_hbm.3) | copy-start | bytes 172036
  40.9 21.8 %all-to-all-start.1 = ((f32[16,32,512]{2,1,0:T(8,128)}), f32[16,32,512]{2,1,0:T(8,128)S(1)}, u32[]{:S(2)}, u32[]{:S(2)}) async-start(f32[16,32,512]{2,1,0:T(8,128)} %copy_out.3), calls=%async_computation.1 | async-start | bytes 2097152 | tf_op jit(solution)/shard_map/all_to_all | solution.py:358
  62.7 18.9 %all-to-all-start.2 = ((f32[16,28,512]{2,1,0:T(8,128)}), f32[16,28,512]{2,1,0:T(8,128)S(1)}, u32[]{:S(2)}, u32[]{:S(2)}) async-start(f32[16,28,512]{2,1,0:T(8,128)} %copy_out.2), calls=%async_computation.2 | async-start | bytes 2097152 | tf_op jit(solution)/shard_map/all_to_all | solution.py:360
Sparse Core Ops, SparseCore 0:
  10.7 77.7 all-gather.2

commit v9 on v8

--- a/solution.py
+++ b/solution.py
@@ -289,19 +289,21 @@
     for i in (0, 1):
         loads[i].start()
     loads[0].wait()
-    for i in (4, 2, 3, 5, 6):
+    for i in (2, 3, 4, 6, 5):
         loads[i].start()
     unpack(0, 10)
     loads[1].wait()
     value = product(0, 256)
     unpack(10, 19)
-    for i in (4, 2, 3, 5, 6):
+    for i in (2, 3):
+        loads[i].wait()
+    later = product(256, 512)
+    unpack(19, 32)
+    columns = halves(truth[...].T[0:320, :])
+    for i in (4, 6, 5):
         loads[i].wait()
     finish(0, 256, value)
-    value = product(256, 512)
-    unpack(19, 32)
-    columns = halves(truth[...].T[0:320, :])
-    finish(256, 512, value)
+    finish(256, 512, later)
     value = product(512, 768)
     send(0, 256)
     send(256, 512)

time: 102 us -> 102 us (level)
  no operation moved by 1% of the time
where the time goes in v9:
time: 102 us; the launch traced here: 101 us
  blocking collectives  29.6 us (29%)
  Pallas kernels  27.3 us (27%)
  waiting for transfers between devices  17.6 us (17%)
  between operations  14.1 us (14%)
  starting transfers between devices  11.1 us (11%)
  local copies, waits for them, and re-layouts  1.5 us (1%)
    all_to_all x1, blocking collectives, per_device(): pieces = lax.all_to_all(small, columns, 0, 0)  29.6 us
    all_to_all x1, waiting for transfers between devices, per_device(): whole = lax.all_to_all(copy_out(strip), rows, 0, 0).reshape(512, 512)  13.9 us
    pallas_call x1, Pallas kernels, invert_factor(): pl.pallas_call(invert_kernel, out_shape=jax.ShapeDtypeStruct((n, n), jnp....  13.5 us
    all_to_all x1, starting transfers between devices, per_device(): whole = lax.all_to_all(copy_out(strip), rows, 0, 0).reshape(512, 512)  6.76 us
    pallas_call x1, Pallas kernels, apply_inverse(): pl.pallas_call(apply_kernel, out_shape=(jax.ShapeDtypeStruct((448, 896),...  5.93 us
    all_to_all x1, starting transfers between devices, per_device(): dealt = lax.all_to_all(copies, rows, 0, 0)  4.31 us
    pallas_call x1, Pallas kernels, solve_dealt(): pl.pallas_call(dealt_kernel, out_shape=(half, half, jax.ShapeDtypeStruct(...  4.2 us
    all_gather x1, waiting for transfers between devices, per_device(): gathered = lax.all_gather(packed, columns, axis=0, tiled=False)  2.59 us
  transfers between devices with their start and end apart: 3, of which 3 were waited for; matrix products, arithmetic and copies ran while one was open for 1% of the time, Pallas kernels for 20%

profile of v9, /device:TPU:1, one launch (start us, length us, event | category | flops | bytes accessed | tf_op | source)
XLA Modules:
  0.0 101.2 jit_solution(7048034276632830639)
XLA Ops:
  7.2 0.0 all-gather.3.cloned.1.call-start
  7.2 1.5 %pack.1 = f32[40,512]{1,0:T(8,128)} custom-call(f32[28,512]{1,0:T(8,128)} %panel_hbm.3, f32[16,320]{1,0:T(8,128)} %bitcast.14), custom_call_target="tpu_custom_call" | custom-call | tf_op jit(solution)/shard_map/pack/pallas_call | solution.py:153
  8.7 0.0 all-gather.3.cloned.1.call-update
  8.7 0.8 copy.11
  9.5 0.1 broadcast_in_dim.10
  9.6 29.6 %all_to_all.15 = f32[32,4,128]{2,1,0:T(4,128)S(1)} all-to-all(f32[32,4,128]{2,1,0:T(4,128)S(1)} %broadcast_in_dim.11), channel_id=1, replica_groups=mesh['x'=4,'y'=4,'z'=16,'k'=2] {'z','k'}, dimensions={0} | all-to-all | bytes 131072 | tf_op jit(solution)/shard_map/all_to_all | solution.py:358
  39.2 0.1 copy.12
  39.3 0.2 copy.13
  39.5 0.3 reshape.20.strip_ref
  39.8 0.0 copy-start
  39.8 1.1 %copy_out.3 = f32[16,32,512]{2,1,0:T(8,128)} custom-call(f32[32,512]{1,0:T(8,128)S(1)} %reshape.20.strip_ref), custom_call_target="tpu_custom_call" | custom-call | tf_op jit(solution)/shard_map/copy_out/pallas_call | solution.py:178
  40.9 6.8 %all-to-all-start.1 = ((f32[16,32,512]{2,1,0:T(8,128)}), f32[16,32,512]{2,1,0:T(8,128)S(1)}, u32[]{:S(2)}, u32[]{:S(2)}) async-start(f32[16,32,512]{2,1,0:T(8,128)} %copy_out.3), calls=%async_computation.1 | async-start | bytes 2097152 | tf_op jit(solution)/shard_map/all_to_all | solution.py:360
  47.7 0.0 copy-done
  47.7 1.1 %copy_out.2 = f32[16,28,512]{2,1,0:T(8,128)} custom-call(f32[28,512]{1,0:T(8,128)S(1)} %copy-done), custom_call_target="tpu_custom_call" | custom-call | tf_op jit(solution)/shard_map/copy_out/pallas_call | solution.py:178
  48.8 13.9 %all-to-all-done.1 = f32[16,32,512]{2,1,0:T(8,128)S(1)} async-done(((f32[16,32,512]{2,1,0:T(8,128)}), f32[16,32,512]{2,1,0:T(8,128)S(1)}, u32[]{:S(2)}, u32[]{:S(2)}) %all-to-all-start.1) | async-done | bytes 1048608 | tf_op jit(solution)/shard_map/all_to_all | solution.py:360
  62.7 4.3 %all-to-all-start.2 = ((f32[16,28,512]{2,1,0:T(8,128)}), f32[16,28,512]{2,1,0:T(8,128)S(1)}, u32[]{:S(2)}, u32[]{:S(2)}) async-start(f32[16,28,512]{2,1,0:T(8,128)} %copy_out.2), calls=%async_computation.2 | async-start | bytes 2097152 | tf_op jit(solution)/shard_map/all_to_all | solution.py:362
  67.0 13.5 %invert_factor.1.inverse_any = f32[512,512]{1,0:T(8,128)S(1)} custom-call(f32[512,512]{1,0:T(8,128)S(1)} %bitcast.12), custom_call_target="tpu_custom_call" | custom-call | flops 10000000000 | bytes 2000000 | tf_op jit(solution)/shard_map/invert_factor/pallas_call | solution.py:113
  80.5 1.1 %all-to-all-done.2.dealt_any = f32[16,28,512]{2,1,0:T(8,128)S(1)} async-done(((f32[16,28,512]{2,1,0:T(8,128)}), f32[16,28,512]{2,1,0:T(8,128)S(1)}, u32[]{:S(2)}, u32[]{:S(2)}) %all-to-all-start.2) | async-done | bytes 917536 | tf_op jit(solution)/shard_map/all_to_all | solution.py:362
  81.6 4.2 %solve_dealt.1 = (bf16[448,512]{1,0:T(8,128)(2,1)S(1)}, bf16[448,512]{1,0:T(8,128)(2,1)S(1)}, f32[28,512]{1,0:T(8,128)}) custom-call(f32[512,512]{1,0:T(8,128)S(1)} %invert_factor.1.inverse_any, f32[16,28,512]{2,1,0:T(8,128)S(1)} %all-to-all-done.2.dealt_any, f32[28,512]{1,0:T(8,128)} %panel_hbm.3), custom_call_target="tpu_custom_call" | custom-call | flops 1000000000 | bytes 2000000 | tf_op jit(solution)/shard_map/solve_dealt/pallas_call | solution.py:227
  85.8 2.6 %all-gather.3.cloned.1.call-done = f32[1280,512]{1,0:T(8,128)} async-done(((f32[40,512]{1,0:T(8,128)}), f32[1280,512]{1,0:T(8,128)}) %all-gather.3.cloned.1.call-update) | async-done | bytes 2621456 | tf_op jit(solution)/shard_map/all_gather | solution.py:356
  88.4 5.9 %apply_inverse.1 = (f32[448,896]{1,0:T(8,128)}, f32[16,320]{1,0:T(8,128)}, f32[320,448]{1,0:T(8,128)}) custom-call(s32[1]{0:T(128)} %bitcast.3.col_ref, f32[512,512]{1,0:T(8,128)S(1)} %invert_factor.1.inverse_any, bf16[448,512]{1,0:T(8,128)(2,1)S(1)} %get-tuple-element.15.w_high, bf16[448,512]{1,0:T(8,128)(2,1)S(1)} %get-tuple-element.16.w_low, ...), custom_call_target="tpu_custom_call" | custom-call | flops 4000000000 | bytes 10000000 | tf_op jit(solution)/shard_map/apply_inverse/pallas_call | solution.py:327
  (1 shorter events, 0.0 us)
Async XLA Ops:
  7.2 81.3 %all-gather.3.cloned.1.call-start = ((), (), s32[]{:S(2)}) async-start(), calls=%async_computation.3 | async-start | bytes 2703360 | tf_op jit(solution)/shard_map/all_gather | solution.py:356
  39.8 7.9 %copy-start = (f32[28,512]{1,0:T(8,128)S(1)}, f32[28,512]{1,0:T(8,128)}, u32[]{:S(2)}) copy-start(f32[28,512]{1,0:T(8,128)} %panel_hbm.3) | copy-start | bytes 172036
  40.9 21.8 %all-to-all-start.1 = ((f32[16,32,512]{2,1,0:T(8,128)}), f32[16,32,512]{2,1,0:T(8,128)S(1)}, u32[]{:S(2)}, u32[]{:S(2)}) async-start(f32[16,32,512]{2,1,0:T(8,128)} %copy_out.3), calls=%async_computation.1 | async-start | bytes 2097152 | tf_op jit(solution)/shard_map/all_to_all | solution.py:360
  62.7 18.9 %all-to-all-start.2 = ((f32[16,28,512]{2,1,0:T(8,128)}), f32[16,28,512]{2,1,0:T(8,128)S(1)}, u32[]{:S(2)}, u32[]{:S(2)}) async-start(f32[16,28,512]{2,1,0:T(8,128)} %copy_out.2), calls=%async_computation.2 | async-start | bytes 2097152 | tf_op jit(solution)/shard_map/all_to_all | solution.py:362
Sparse Core Ops, SparseCore 0:
  10.7 77.7 all-gather.2
